TPU v7x, 128 devices: a whole 4x4x4 slice. The times are simulated.
128 devices in a mesh: seq: 64 (over y, z, x), head: 2 (over core).
Axes of the slice: x: 4, y: 4, z: 4, core: 2. Of those that a mesh axis runs over, the one named last changes fastest.
Arguments:
- queries: bfloat16 [32768, 2048], P('seq', 'head'), may hold values from -60 to 60
- keys: bfloat16 [32768, 2048], P('seq', 'head'), may hold values from -6 to 6
- values: bfloat16 [32768, 2048], P('seq', 'head'), may hold values from -6 to 6
- out_grad: bfloat16 [32768, 2048], P('seq', 'head'), may hold values from -6 to 6
- rand_ids: int32 [16, 256, 3], replicated, may hold values from 0 to 255, as said below
- glob_ids: int32 [2], replicated, may hold values from 0 to 255, as said below
Outputs:
- out: bfloat16 [32768, 2048], P('seq', 'head')
- query_gradient: bfloat16 [32768, 2048], P('seq', 'head')
- key_grad: bfloat16 [32768, 2048], P('seq', 'head')
- value_grad: bfloat16 [32768, 2048], P('seq', 'head')
Inputs may be any that keep to these rules, and one draw needn't show every extreme that they name: `rand_ids`: group the heads into runs of 8 and the query blocks into runs of 4; within one head run and one query run, the entries name key blocks of any one aligned run of 4 blocks (blocks 4j to 4j + 3, those of one index of seq) at most 2 times, and exactly 2 times for some such run. `glob_ids`: the ids are distinct, and one of them is the last block, 255.
All inputs are finite; a program needn't handle non-finite values.
Results may differ from a plain program's by a relative error of at most 0.014.
Values may be sent and summed in bfloat16 or wider, within the bound.
A program may use at most 128 MiB of HBM per device.

v0:
```python
import math

import jax
import jax.numpy as jnp
from jax import lax
from jax.sharding import PartitionSpec as P

BLOCK = 128
DH = 128
RAND = 3
GLOB = 2
WMAX = 1


masked_value = -1e30


def with_halo(block, sides, width):
    for axis, dim in sides:
        count = lax.axis_size(axis)
        forward = [(i, i + 1) for i in range(count - 1)]
        backward = [(target, source) for source, target in forward]
        low = lax.ppermute(
            lax.slice_in_dim(block, block.shape[dim] - width, None, axis=dim), axis, forward
        )
        high = lax.ppermute(lax.slice_in_dim(block, 0, width, axis=dim), axis, backward)
        block = jnp.concatenate([low, block, high], axis=dim)
    return block


def spread_2(array, axis, root):
    mine = lax.axis_index(axis) == root
    return lax.psum(jnp.where(mine, array, jnp.zeros_like(array)), axis)


def from_behind(value, axis, steps):
    count = lax.axis_size(axis)
    initial, last = (max(0, -steps), min(count, count - steps))
    return lax.ppermute(value, axis, [(source, source + steps) for source in range(initial, last)])


def body(queries, keys, values, out_grad, rand_ids, glob_ids):
    block_size = BLOCK
    head_size = DH
    half_width = WMAX
    rand_count = RAND
    glob_count = GLOB
    window_span = 2 * half_width + 1
    rows_here = queries.shape[0]
    heads_here = queries.shape[1] // head_size
    blocks_here = rows_here // block_size
    shards = lax.axis_size("seq")
    place = lax.axis_index("seq")
    group = lax.axis_index("head")
    all_blocks = blocks_here * shards
    score_scale = 1.0 / math.sqrt(head_size)

    def to_heads(array):
        return array.reshape(blocks_here, block_size, heads_here, head_size).transpose(2, 0, 1, 3)

    def from_heads(array):
        return array.transpose(1, 2, 0, 3).reshape(rows_here, heads_here * head_size)

    kv_pair = jnp.stack([keys, values])
    banded = with_halo(kv_pair, (("seq", 1),), half_width * block_size)
    band_pair = banded.reshape(
        2, blocks_here + 2 * half_width, block_size, heads_here, head_size
    ).transpose(3, 0, 1, 2, 4)
    pieces = []
    for glob_number in range(glob_count):
        owner_index = glob_ids[glob_number] // blocks_here
        local_block = glob_ids[glob_number] - owner_index * blocks_here
        piece = lax.dynamic_slice_in_dim(kv_pair, local_block * block_size, block_size, 1)
        pieces.append(spread_2(piece, "seq", owner_index))
    glob_pair = (
        jnp.stack(pieces)
        .reshape(glob_count, 2, block_size, heads_here, head_size)
        .transpose(3, 1, 0, 2, 4)
    )
    rows_per = heads_here * blocks_here * rand_count
    cap = max(2, (5 * rows_per + 4 * shards - 1) // (4 * shards))
    ids_mine = lax.dynamic_slice_in_dim(rand_ids, group * heads_here, heads_here, 0)
    requests = (
        ids_mine.reshape(heads_here, shards, blocks_here, rand_count)
        .transpose(1, 0, 2, 3)
        .reshape(shards, rows_per)
    )
    source = requests // blocks_here
    source_hits = (source[:, :, None] == jnp.arange(shards, dtype=jnp.int32)[None, None, :]).astype(
        jnp.int32
    )
    earlier = jnp.cumsum(source_hits, axis=1) - source_hits
    slot_index = jnp.sum(earlier * source_hits, axis=2)
    own_source = lax.dynamic_index_in_dim(source, place, 0, False)
    own_slot = lax.dynamic_index_in_dim(slot_index, place, 0, False)
    pick_index = own_source * cap + own_slot
    head_of = jnp.arange(rows_per, dtype=jnp.int32) // (blocks_here * rand_count)
    flat_index = (requests - place * blocks_here) * heads_here + head_of[None, :]
    slot_match = (source == place)[:, :, None] & (
        slot_index[:, :, None] == jnp.arange(cap, dtype=jnp.int32)[None, None, :]
    )
    send_index = jnp.sum(jnp.where(slot_match, flat_index[:, :, None], 0), axis=1)
    send_live = jnp.any(slot_match, axis=1)
    block_table = kv_pair.reshape(2, blocks_here, block_size, heads_here, head_size).transpose(
        1, 3, 0, 2, 4
    )
    block_table = block_table.reshape(blocks_here * heads_here, 2, block_size, head_size)
    payload = block_table[send_index]
    chosen = lax.all_to_all(payload, "seq", split_axis=0, concat_axis=0, tiled=True).reshape(
        shards * cap, 2, block_size, head_size
    )[pick_index]
    chosen = chosen.reshape(heads_here, blocks_here, rand_count, 2, block_size, head_size)
    fetched = chosen.transpose(0, 3, 1, 2, 4, 5)
    offsets = jnp.arange(window_span, dtype=jnp.int32) - half_width
    positions = (
        place * blocks_here + jnp.arange(blocks_here, dtype=jnp.int32)[:, None] + offsets[None, :]
    )
    inside = (positions >= 0) & (positions < all_blocks)
    live_window = jnp.broadcast_to(inside[None], (heads_here, blocks_here, window_span))
    live_mask = jnp.concatenate(
        [live_window, jnp.ones((heads_here, blocks_here, rand_count + glob_count), bool)], axis=2
    )

    def gathered_key_blocks(band_head, rand_head, glob_head):
        windowed = jnp.stack(
            [band_head[:, offset : offset + blocks_here] for offset in range(window_span)], axis=2
        )
        spread = jnp.broadcast_to(
            glob_head[:, None], (2, blocks_here, glob_count, block_size, head_size)
        )
        return jnp.concatenate([windowed, rand_head, spread], axis=2)

    def softmax_weights(query_per_head, listed_blocks, live_head):
        unscaled_scores = (
            jnp.einsum(
                "zjs,zcls->zjcl",
                query_per_head,
                listed_blocks[0],
                preferred_element_type=jnp.float32,
            )
            * score_scale
        )
        unscaled_scores = jnp.where(live_head[:, None, :, None], unscaled_scores, masked_value)
        peak = jnp.max(unscaled_scores, axis=(2, 3), keepdims=True)
        exponent = jnp.exp(unscaled_scores - peak)
        return exponent / jnp.sum(exponent, axis=(2, 3), keepdims=True)

    def forward_head(operands):
        query_per_head, band_head, rand_head, glob_head, live_head = operands
        listed_blocks = gathered_key_blocks(band_head, rand_head, glob_head)
        weights_narrow_float = softmax_weights(query_per_head, listed_blocks, live_head).astype(
            jnp.bfloat16
        )
        result = jnp.einsum(
            "qhgf,qgfm->qhm",
            weights_narrow_float,
            listed_blocks[1],
            preferred_element_type=jnp.float32,
        )
        return result.astype(jnp.bfloat16)

    query_heads = to_heads(queries)
    grad_heads = to_heads(out_grad)
    out_heads = lax.map(forward_head, (query_heads, band_pair, fetched, glob_pair, live_mask))

    def backward_head(operands):
        (
            query_per_head,
            band_head,
            rand_head,
            glob_head,
            live_head,
            gradient_per_head,
            output_per_head,
        ) = operands
        listed_blocks = gathered_key_blocks(band_head, rand_head, glob_head)
        weights = softmax_weights(query_per_head, listed_blocks, live_head)
        weights_narrow_float = weights.astype(jnp.bfloat16)
        row_delta = jnp.sum(
            gradient_per_head.astype(jnp.float32) * output_per_head.astype(jnp.float32), axis=-1
        )
        probability_gradient = jnp.einsum(
            "zjs,zcls->zjcl",
            gradient_per_head,
            listed_blocks[1],
            preferred_element_type=jnp.float32,
        )
        score_narrow_float = (
            weights * (probability_gradient - row_delta[:, :, None, None])
        ).astype(jnp.bfloat16)
        query_gradient = (
            jnp.einsum(
                "qhgf,qgfm->qhm",
                score_narrow_float,
                listed_blocks[0],
                preferred_element_type=jnp.float32,
            )
            * score_scale
        )
        key_gradient_parts = (
            jnp.einsum(
                "yelt,yev->yltv",
                score_narrow_float,
                query_per_head,
                preferred_element_type=jnp.float32,
            )
            * score_scale
        )
        value_gradient_parts = jnp.einsum(
            "yelt,yev->yltv",
            weights_narrow_float,
            gradient_per_head,
            preferred_element_type=jnp.float32,
        )
        terms = jnp.stack([key_gradient_parts, value_gradient_parts])
        band_sum = jnp.zeros((2, blocks_here + 2 * half_width, block_size, head_size), jnp.float32)
        for offset in range(window_span):
            band_sum = band_sum + jnp.pad(
                terms[:, :, offset], ((0, 0), (offset, window_span - 1 - offset), (0, 0), (0, 0))
            )
        rand_part = terms[:, :, window_span : window_span + rand_count].astype(jnp.bfloat16)
        glob_part = jnp.sum(terms[:, :, window_span + rand_count :], axis=1)
        return (query_gradient.astype(jnp.bfloat16), band_sum, rand_part, glob_part)

    query_grads, band_sums, rand_terms, glob_terms = lax.map(
        backward_head,
        (query_heads, band_pair, fetched, glob_pair, live_mask, grad_heads, out_heads),
    )
    center = band_sums[:, :, half_width : half_width + blocks_here]
    for shift_by in (1, -1):
        if shift_by == 1:
            rim_terms = band_sums[:, :, blocks_here + half_width :]
        else:
            rim_terms = band_sums[:, :, :half_width]
        moved_rim = from_behind(rim_terms, "seq", shift_by)
        if shift_by == 1:
            center = center.at[:, :, :half_width].add(moved_rim)
        else:
            center = center.at[:, :, blocks_here - half_width :].add(moved_rim)
    glob_total = lax.psum(glob_terms, "seq")
    owned_mask = (
        glob_ids[:, None] == place * blocks_here + jnp.arange(blocks_here, dtype=jnp.int32)[None, :]
    ).astype(jnp.float32)
    center = center + jnp.einsum(
        "gi,hcgbd->hcibd", owned_mask, glob_total, precision=lax.Precision.HIGHEST
    )
    outgoing_terms = rand_terms.transpose(0, 2, 3, 1, 4, 5).reshape(
        rows_per, 2, block_size, head_size
    )
    outgoing = (
        jnp.zeros((shards * cap, 2, block_size, head_size), jnp.bfloat16)
        .at[pick_index]
        .set(outgoing_terms)
    )
    outgoing = outgoing.reshape(shards, cap, 2, block_size, head_size)
    returned = lax.all_to_all(outgoing, "seq", split_axis=0, concat_axis=0, tiled=True)
    target = jnp.where(send_live, send_index, blocks_here * heads_here).reshape(-1)
    gathered = (
        jnp.zeros((blocks_here * heads_here, 2, block_size, head_size), jnp.float32)
        .at[target]
        .add(
            returned.reshape(shards * cap, 2, block_size, head_size).astype(jnp.float32),
            mode="drop",
        )
    )
    center = center + gathered.reshape(blocks_here, heads_here, 2, block_size, head_size).transpose(
        1, 2, 0, 3, 4
    )
    key_grad = from_heads(center[:, 0].astype(jnp.bfloat16))
    value_grad = from_heads(center[:, 1].astype(jnp.bfloat16))
    return (from_heads(out_heads), from_heads(query_grads), key_grad, value_grad)


def solution(mesh):
    return jax.shard_map(
        body,
        mesh=mesh,
        in_specs=(P("seq", "head"), P("seq", "head"), P("seq", "head"), P("seq", "head"), P(), P()),
        out_specs=(P("seq", "head"), P("seq", "head"), P("seq", "head"), P("seq", "head")),
        check_vma=False,
    )
```

profile of v0, /device:TPU:54, one launch (start us, length us, event | category | flops | bytes accessed | tf_op | source)
XLA Modules:
  0.0 749.2 jit_solution(7130629682425746473)
XLA Ops:
  8.6 3.3 fusion.58
  13.9 6.5 gather_fusion
  20.4 11.2 %all-to-all-start = ((bf16[64,2,2,128,128]{4,3,2,1,0:T(8,128)(2,1)}), bf16[64,2,2,128,128]{4,3,2,1,0:T(8,128)(2,1)}, u32[]{:S(2)}, u32[]{:S(2)}) async-start(bf16[64,2,2,128,128]{4,3,2,1,0:T(8,128)(2,1)} %bitcast.332), calls=%async_computation | async-start | bytes 16777216 | tf_op jit(solution)/shard_map/all_to_all | solution.py:109
  42.9 3.5 collective-permute-start
  46.4 2.5 collective-permute-start.1
  52.9 90.8 %collective-permute-done = bf16[2,128,1024]{1,2,0:T(8,128)(2,1)} collective-permute-done((bf16[2,128,1024]{1,2,0:T(8,128)(2,1)}, bf16[2,128,1024]{1,2,0:T(8,128)(2,1)}, u32[]{:S(2)}, u32[]{:S(2)}) %collective-permute-start) | collective-permute-done | bytes 524320 | tf_op jit(solution)/shard_map/ppermute | solution.py:23
  143.6 5.0 collective-permute-done.1
  150.8 2.9 copy.202
  153.7 2.7 copy.252
  157.2 96.9 %all-reduce.10.cloned.1.call-done = (bf16[1,2,128,8,128]{2,4,3,1,0:T(8,128)(2,1)}, bf16[1,2,128,8,128]{2,4,3,1,0:T(8,128)(2,1)}) async-done(((bf16[1,2,128,8,128]{2,4,3,1,0:T(8,128)(2,1)}, bf16[1,2,128,8,128]{2,4,3,1,0:T(8,128)(2,1)}), (bf16[1,2,128,8,128]{2,4,3,1,0:T(8,128)(2,1)}, bf16[1,2,128,8,128]{2,4,3,1,0:T(8,128)(2,1)})) %all-reduce.10.cloned.1.call-update) | async-done | bytes 1048592 | tf_op jit(solution)/shard_map/psum | solution.py:33
  256.3 2.3 copy.218
  258.6 9.4 %gather_fusion.1 = bf16[96,2,128,128]{3,2,1,0:T(8,128)(2,1)} fusion(bf16[128,2,128,128]{3,2,1,0:T(8,128)(2,1)} %bitcast.58, s32[1024]{0:T(1024)S(1)} %pad_clamp_fusion), kind=kCustom, calls=%fused_computation.1 | custom fusion | bytes 12583296 | tf_op jit(solution)/shard_map/gather | solution.py:109
  268.0 8.1 %copy.217 = bf16[8,2,4,3,128,128]{5,4,3,2,1,0:T(8,128)(2,1)} copy(bf16[8,2,4,3,128,128]{5,4,1,3,2,0:T(8,128)(2,1)} %bitcast.334) | data formatting | bytes 12582912 | tf_op jit(solution)/shard_map/while | solution.py:164
  277.3 47.6 %while.30 = (s32[]{:T(128)}, bf16[8,4,128,128]{3,2,1,0:T(8,128)(2,1)}, pred[8,4,8]{2,1,0:T(4,128)(4,1)S(1)}, bf16[8,4,128,128]{3,2,1,0:T(8,128)(2,1)}, bf16[8,2,...) while((s32[]{:T(128)}, ...), condition=%wide.region_8.9_spmd, body=%wide.region_5.8_spmd.sunk | while | flops 274791424 | bytes 13512901 | solution.py:164
  326.2 116.4 %while.31 = (s32[]{:T(128)}, bf16[8,4,128,128]{3,2,1,0:T(8,128)(2,1)}, f32[8,2,6,128,128]{4,3,2,1,0:T(8,128)}, bf16[8,2,4,3,128,128]{5,4,1,3,2,0:T(8,128)(2,1)},...) while((s32[]{:T(128)}, ...), condition=%wide.region_14.15_spmd, body=%wide.region_9.14_spmd.sunk | while | flops 683604480 | bytes 42753296 | solution.py:225
  442.5 5.3 broadcast_in_dim.151
  447.9 17.8 %scatter_fusion = bf16[128,2,128,128]{3,2,1,0:T(8,128)(2,1)} fusion(bf16[128,2,128,128]{3,2,1,0:T(8,128)(2,1)} %broadcast_in_dim.151, s32[96]{0:T(128)S(1)} %fusion.75, bf16[96,2,128,128]{3,2,1,0:T(8,128)(2,1)} %bitcast.341), kind=kCustom, calls=%fused_computation.2 | custom fusion | bytes 18874752 | tf_op jit(solution)/shard_map/scatter | solution.py:253
  465.6 10.4 %all-to-all-start.1 = ((bf16[64,2,2,128,128]{4,3,2,1,0:T(8,128)(2,1)}), bf16[64,2,2,128,128]{4,3,2,1,0:T(8,128)(2,1)}, u32[]{:S(2)}, u32[]{:S(2)}) async-start(bf16[64,2,2,128,128]{4,3,2,1,0:T(8,128)(2,1)} %bitcast.330), calls=%async_computation.1 | async-start | bytes 16777216 | tf_op jit(solution)/shard_map/all_to_all | solution.py:256
  476.1 3.5 fusion.79
  479.6 3.4 collective-permute-start.2
  483.0 2.5 collective-permute-start.3
  485.8 7.4 copy.226
  493.2 3.1 slice.214
  502.0 109.8 %collective-permute-done.2 = f32[8,2,1,128,128]{4,2,3,1,0:T(1,128)S(1)} collective-permute-done((f32[8,2,1,128,128]{4,2,3,1,0:T(1,128)}, f32[8,2,1,128,128]{4,2,3,1,0:T(1,128)S(1)}, u32[]{:S(2)}, u32[]{:S(2)}) %collective-permute-start.2) | collective-permute-done | bytes 1048608 | tf_op jit(solution)/shard_map/ppermute | solution.py:39
  612.7 2.3 add.204
  615.0 28.6 %scatter-add.14 = f32[8,2,4,128,128]{4,2,3,1,0:T(4,128)} dynamic-update-slice(f32[8,2,4,128,128]{4,2,3,1,0:T(4,128)} %slice.214, f32[8,2,1,128,128]{4,2,3,1,0:T(1,128)S(1)} %add.204, s32[]{:T(128)} %constant.208.clone.1, s32[]{:T(128)} %constant.208.clone.1, s32[]{:T(128)} %constant.208.clone.1, s32[]{:T(128)} %constant.208.clone.1, s32[]{:T(128)} %constant.208.clone.1) | dynamic-update-slice | bytes 2097156 | tf_op jit(solution)/shard_map/scatter-add | solution.py:237
  643.6 3.8 slice_add_fusion
  647.4 28.2 %scatter-add.18 = f32[8,2,4,128,128]{4,2,3,1,0:T(4,128)} dynamic-update-slice(f32[8,2,4,128,128]{4,2,3,1,0:T(4,128)} %scatter-add.14, f32[8,2,1,128,128]{4,2,3,1,0:T(1,128)S(1)} %slice_add_fusion, s32[]{:T(128)} %constant.208.clone.1, s32[]{:T(128)} %constant.208.clone.1, s32[]{:T(128)} %constant.214.clone.1, s32[]{:T(128)} %constant.208.clone.1, s32[]{:T(128)} %constant.208.clone.1) | dynamic-update-slice | bytes 2097156 | tf_op jit(solution)/shard_map/scatter-add | solution.py:239
  675.6 11.6 %bitcast_convert_fusion = f32[128,2,128,128]{3,2,1,0:T(8,128)} fusion(bf16[64,2,2,128,128]{4,3,2,1,0:T(8,128)(2,1)} %all-to-all-done.1), kind=kLoop, calls=%fused_computation.100 | loop fusion | flops 4194304 | bytes 25165824 | tf_op jit(solution)/shard_map/convert_element_type | solution.py:262
  687.2 2.4 broadcast_in_dim.150
  689.7 37.2 %scatter_fusion.1 = f32[32,2,128,128]{3,2,1,0:T(8,128)} fusion(f32[32,2,128,128]{3,2,1,0:T(8,128)} %broadcast_in_dim.150, s32[128]{0:T(128)S(1)} %fusion.76, f32[128,2,128,128]{3,2,1,0:T(8,128)} %bitcast_convert_fusion), kind=kCustom, calls=%fused_computation.3 | custom fusion | flops 4194304 | bytes 50332160 | tf_op jit(solution)/shard_map/scatter-add | solution.py:261
  726.9 11.2 %fusion.56 = bf16[8,2,4,128,128]{4,2,3,1,0:T(4,128)(2,1)S(1)} fusion(f32[8,2,4,128,128]{4,2,3,1,0:T(4,128)} %scatter-add.18, f32[4,8,2,128,128]{4,3,2,1,0:T(8,128)} %bitcast.329, f32[8,2,2,128,128]{4,2,3,1,0:T(2,128)} %all-reduce.8.cloned.1.call-done, s32[4]{0:T(128)S(1)} %copy-done.16, s32[2]{0:T(128)S(1)} %copy-done.14), kind=kOutput, calls=%fused_computation.105 | convolution fusion | flops 28311560 | bytes 12582936 | tf_op jit(solution)/shard_map/gi,hcgbd->hcibd/dot_general | solution.py:244
  (347 shorter events, 193.1 us)
Async XLA Ops:
  7.2 0.8 copy-start
  7.2 5.4 copy-start.4
  7.2 5.7 copy-start.5
  8.5 4.1 copy-start.9
  12.3 0.9 copy-start.11
  20.4 11.3 %copy-start.13 = (s32[2]{0:T(128)S(1)}, s32[2]{0:T(128)}, u32[]{:S(2)}) copy-start(s32[2]{0:T(128)} %param.19) | copy-start | bytes 28
  20.4 238.2 %all-to-all-start = ((bf16[64,2,2,128,128]{4,3,2,1,0:T(8,128)(2,1)}), bf16[64,2,2,128,128]{4,3,2,1,0:T(8,128)(2,1)}, u32[]{:S(2)}, u32[]{:S(2)}) async-start(bf16[64,2,2,128,128]{4,3,2,1,0:T(8,128)(2,1)} %bitcast.332), calls=%async_computation | async-start | bytes 16777216 | tf_op jit(solution)/shard_map/all_to_all | solution.py:109
  31.7 222.4 %all-reduce.10.cloned.1.call-start = ((), (), s32[]{:S(2)}) async-start(), calls=%async_computation.3 | async-start | bytes 2097152 | tf_op jit(solution)/shard_map/psum | solution.py:33
  39.4 3.4 copy-start.2
  41.3 1.7 copy-start.3
  41.3 7.6 %copy-start.7 = (bf16[512,1024]{1,0:T(8,128)(2,1)S(1)}, bf16[512,1024]{1,0:T(8,128)(2,1)}, u32[]{:S(2)}) copy-start(bf16[512,1024]{1,0:T(8,128)(2,1)} %param.14) | copy-start | bytes 3145732
  42.9 6.3 copy-start.8
  42.9 100.7 %collective-permute-start = (bf16[2,128,1024]{1,2,0:T(8,128)(2,1)}, bf16[2,128,1024]{1,2,0:T(8,128)(2,1)}, u32[]{:S(2)}, u32[]{:S(2)}) collective-permute-start(bf16[2,128,1024]{1,2,0:T(8,128)(2,1)} %get-tuple-element.372), channel_id=1, source_target_pairs={{0,2},{2,4},{4,6},{6,8},{8,10},{10,12},{12,14},{14,16},{16,18},{18... | collective-permute-start | bytes 1572872 | tf_op jit(solution)/shard_map/ppermute | solution.py:23
  46.4 102.2 %collective-permute-start.1 = (bf16[2,128,1024]{1,2,0:T(8,128)(2,1)}, bf16[2,128,1024]{1,2,0:T(8,128)(2,1)}, u32[]{:S(2)}, u32[]{:S(2)}) collective-permute-start(bf16[2,128,1024]{1,2,0:T(8,128)(2,1)} %get-tuple-element.373), channel_id=1, source_target_pairs={{2,0},{4,2},{6,4},{8,6},{10,8},{12,10},{14,12},{16,14},{18,16},{20... | collective-permute-start | bytes 1572872 | tf_op jit(solution)/shard_map/ppermute | solution.py:26
  52.1 0.6 copy-start.15
  465.6 210.0 %all-to-all-start.1 = ((bf16[64,2,2,128,128]{4,3,2,1,0:T(8,128)(2,1)}), bf16[64,2,2,128,128]{4,3,2,1,0:T(8,128)(2,1)}, u32[]{:S(2)}, u32[]{:S(2)}) async-start(bf16[64,2,2,128,128]{4,3,2,1,0:T(8,128)(2,1)} %bitcast.330), calls=%async_computation.1 | async-start | bytes 16777216 | tf_op jit(solution)/shard_map/all_to_all | solution.py:256
  476.0 250.8 %all-reduce.8.cloned.1.call-start = ((), (), s32[]{:S(2)}) async-start(), calls=%async_computation.2 | async-start | bytes 4194304 | tf_op jit(solution)/shard_map/psum | solution.py:240
  476.1 9.4 %copy-start.10 = (pred[64,96]{1,0:T(8,128)(4,1)S(1)}, pred[64,96]{1,0:T(8,128)(4,1)}, u32[]{:S(2)}) copy-start(pred[64,96]{1,0:T(8,128)(4,1)} %copy-done.9) | copy-start | bytes 18436
  476.1 9.5 %copy-start.12 = (s32[64,2]{0,1:T(2,128)S(1)}, s32[64,2]{0,1:T(2,128)}, u32[]{:S(2)}) copy-start(s32[64,2]{0,1:T(2,128)} %copy-done.11) | copy-start | bytes 1540
  479.6 132.1 %collective-permute-start.2 = (f32[8,2,1,128,128]{4,2,3,1,0:T(1,128)}, f32[8,2,1,128,128]{4,2,3,1,0:T(1,128)S(1)}, u32[]{:S(2)}, u32[]{:S(2)}) collective-permute-start(f32[8,2,1,128,128]{4,2,3,1,0:T(1,128)} %bitcast.73), channel_id=1, source_target_pairs={{0,2},{2,4},{4,6},{6,8},{8,10},{10,12},{12,14},{14,16},{16,18},{18... | collective-permute-start | bytes 3145736 | tf_op jit(solution)/shard_map/ppermute | solution.py:39
  483.0 160.6 %collective-permute-start.3 = (f32[8,2,1,128,128]{4,2,3,1,0:T(1,128)}, f32[8,2,1,128,128]{4,2,3,1,0:T(1,128)S(1)}, u32[]{:S(2)}, u32[]{:S(2)}) collective-permute-start(f32[8,2,1,128,128]{4,2,3,1,0:T(1,128)} %bitcast.74), channel_id=1, source_target_pairs={{2,0},{4,2},{6,4},{8,6},{10,8},{12,10},{14,12},{16,14},{18,16},{20... | collective-permute-start | bytes 3145736 | tf_op jit(solution)/shard_map/ppermute | solution.py:39
  611.7 1.0 copy-start.6
  689.7 37.2 %copy-start.14 = (s32[2]{0:T(128)S(1)}, s32[2]{0:T(128)}, u32[]{:S(2)}) copy-start(s32[2]{0:T(128)} %param.19) | copy-start | bytes 28
  689.7 37.2 %copy-start.16 = (s32[4]{0:T(128)S(1)}, s32[4]{0:T(128)}, u32[]{:S(2)}) copy-start(s32[4]{0:T(128)} %copy-done.15) | copy-start | bytes 52
  740.3 1.9 copy-start.1
Sparse Core Ops, SparseCore 0:
  49.0 204.9 all-reduce.9
  496.4 201.8 all-reduce.7
where the time goes:
time: 760 us; the launch traced here: 749 us
  waiting for transfers between devices  302 us (40%)
  local copies, waits for them, and re-layouts  199 us (26%)
  other arithmetic  102 us (13%)
  matrix products  90.4 us (12%)
  starting transfers between devices  33.5 us (4%)
  between operations  21.3 us (3%)
    ppermute x2, waiting for transfers between devices, from_behind(): lax.ppermute(value, axis, [(source, source + steps) for source in range(i...  110 us
    psum x1, waiting for transfers between devices, spread_2(): return lax.psum(jnp.where(mine, array, jnp.zeros_like(array)), axis)  96.9 us
    ppermute x1, waiting for transfers between devices, with_halo(): lax.ppermute(lax.slice_in_dim(block, block.shape[dim] - width, None, axis...  90.8 us
    scatter-add x1, other arithmetic, body(): gathered = jnp.zeros((blocks_here * heads_here, 2, block_size, head_size)...  37.2 us
    scatter-add x1, local copies, waits for them, and re-layouts, body(): center = center.at[:, :, :half_width].add(moved_rim)  28.6 us
    scatter-add x1, local copies, waits for them, and re-layouts, body(): center = center.at[:, :, blocks_here - half_width:].add(moved_rim)  28.2 us
    dot_general x16, matrix products, softmax_weights(): jnp.einsum('zjs,zcls->zjcl', query_per_head, listed_blocks[0], preferred_...  21.9 us
    while x64, local copies, waits for them, and re-layouts  21.7 us
  transfers between devices with their start and end apart: 8, of which 4 were waited for; matrix products, arithmetic and copies ran while one was open for 21% of the time, Pallas kernels for 0%

commit v1 on v0

v1 whole, which is shorter than its diff:
```python
import functools
import math

import jax
import jax.numpy as jnp
from jax import lax
from jax.experimental import pallas as pl
from jax.experimental.pallas import tpu as pltpu
from jax.sharding import PartitionSpec as P

BLOCK = 128
DH = 128
RAND = 3
HEADS_HERE = 8
QB = 4
SHARDS = 64
ENTRIES = HEADS_HERE * QB * RAND
NONE = 1 << 20
LAST = SHARDS - 1
GROWS = HEADS_HERE * 2 * BLOCK
PIECE = GROWS // SHARDS
QUART = GROWS // 4
SCALE = 1.0 / math.sqrt(DH)
MASKED = -1e30
MESH = pl.DeviceIdType.MESH
ANY = pl.ANY
BF = jnp.bfloat16
F32 = jnp.float32


def orbits():
    def key(d):
        return (d // 16, (d // 4) % 4, d % 4)

    def hops(d):
        return sum(min(v, 4 - v) for v in key(d))

    seen, rounds = set(), []
    for d in sorted(range(1, SHARDS), key=lambda d: (hops(d), d)):
        if d in seen:
            continue
        orbit = []
        for turn in range(3):
            k = key(d)[turn:] + key(d)[:turn]
            for sign in (1, -1):
                a, b, c = ((sign * v) % 4 for v in k)
                if a * 16 + b * 4 + c not in orbit:
                    orbit.append(a * 16 + b * 4 + c)
        seen.update(orbit)
        rounds.append(orbit)
    return rounds


ROUNDS = orbits()


def moved(me, d, sign=1):
    y, z, x = lax.div(me, 16), lax.rem(lax.div(me, 4), 4), lax.rem(me, 4)
    dy, dz, dx = lax.div(d, 16), lax.rem(lax.div(d, 4), 4), lax.rem(d, 4)
    if sign < 0:
        dy, dz, dx = 4 - dy, 4 - dz, 4 - dx
    return lax.rem(y + dy, 4) * 16 + lax.rem(z + dz, 4) * 4 + lax.rem(x + dx, 4)


def shifted(me, d, sign=1):
    dy, dz, dx = d // 16, (d // 4) % 4, d % 4
    if sign < 0:
        dy, dz, dx = 4 - dy, 4 - dz, 4 - dx
    y, z, x = lax.div(me, 16), lax.rem(lax.div(me, 4), 4), lax.rem(me, 4)
    return lax.rem(y + dy, 4) * 16 + lax.rem(z + dz, 4) * 4 + lax.rem(x + dx, 4)


def remote(src, dst, send, recv, target):
    return pltpu.make_async_remote_copy(
        src_ref=src,
        dst_ref=dst,
        send_sem=send,
        recv_sem=recv,
        device_id={"seq": target},
        device_id_type=MESH,
    )


def enter(me):
    barrier = pltpu.get_barrier_semaphore()

    def greet(d, carry):
        pl.semaphore_signal(
            barrier, inc=1, device_id={"seq": moved(me, d)}, device_id_type=MESH
        )
        return carry

    lax.fori_loop(1, SHARDS, greet, 0)
    pl.semaphore_wait(barrier, SHARDS - 1)


def prep_kernel(cmin, cmax, misc, k_ref, v_ref, payload, cand_o, cand_l, sem, gsem):
    me = lax.axis_index("seq")

    def put(d, carry):
        t = moved(me, d)
        low = cmin[t]
        high = cmax[t]
        for c, code in ((0, jnp.where(low < NONE, low, 0)), (1, jnp.maximum(high, 0))):
            head = lax.div(code, 4 * QB * RAND)
            blk = lax.rem(code, 4)
            rows = pl.ds(pl.multiple_of(blk * BLOCK, BLOCK), BLOCK)
            cols = pl.ds(pl.multiple_of(head * DH, DH), DH)
            pltpu.make_async_copy(k_ref.at[rows, cols], payload.at[d, c, 0], sem).start()
            pltpu.make_async_copy(v_ref.at[rows, cols], payload.at[d, c, 1], sem).start()
        return carry

    rows_o = pl.ds(pl.multiple_of(misc[0] * BLOCK, BLOCK), BLOCK)
    rows_l = pl.ds((QB - 1) * BLOCK, BLOCK)
    for h in range(HEADS_HERE):
        cols = pl.ds(h * DH, DH)
        for kv, ref in ((0, k_ref), (1, v_ref)):
            dst = pl.ds((2 * h + kv) * BLOCK, BLOCK)
            pltpu.make_async_copy(ref.at[rows_o, cols], cand_o.at[dst], gsem.at[0]).start()
            pltpu.make_async_copy(ref.at[rows_l, cols], cand_l.at[dst], gsem.at[1]).start()
    lax.fori_loop(0, SHARDS, put, 0)
    pltpu.make_async_copy(cand_o, cand_o, gsem.at[0]).wait()
    pltpu.make_async_copy(cand_l, cand_l, gsem.at[1]).wait()
    pltpu.make_async_copy(payload, payload, sem).wait()


def send_round(me, sign, src, dst, ss, rs, offsets):
    def piece(i, carry):
        c, kv = lax.div(i, 2), lax.rem(i, 2)
        for d in offsets:
            remote(
                src.at[d, c, kv], dst.at[d, c, kv], ss.at[d], rs.at[d], shifted(me, d, sign)
            ).start()
        return carry

    lax.fori_loop(0, 4, piece, 0)


def sent_round(me, src, dst, ss, rs, offsets):
    for d in offsets:
        remote(src.at[d], dst.at[d], ss.at[d], rs.at[d], me).wait_send()


def arrived_round(me, src, dst, ss, rs, offsets):
    for d in offsets:
        remote(src.at[d], dst.at[d], ss.at[d], rs.at[d], me).wait_recv()


def plane_target(me, dp):
    return shifted(me, dp)


def fetch_kernel(
    sel, payload, k_ref, v_ref, cand_o, cand_l, recv, halo, gfull,
    ay, gq, ap, ss, rs, hs, hr, ys, yr, ps, pr, ls, lr, bs, br, cs, cr, own_sem,
):
    me = lax.axis_index("seq")
    y = lax.div(me, 16)
    plane = lax.rem(me, 16)
    enter(me)
    after = lax.rem(me + 1, SHARDS)
    before = lax.rem(me + SHARDS - 1, SHARDS)
    own = pltpu.make_async_copy(payload.at[0], recv.at[0], own_sem)
    own.start()

    up = []
    for dy in range(1, 4):
        ty = lax.rem(y + dy, 4)
        copy = remote(
            cand_o.at[pl.ds(pl.multiple_of(ty * QUART, QUART), QUART)],
            ay.at[dy], ys.at[dy], yr.at[dy], ty * 16 + plane,
        )
        copy.start()
        up.append(copy)

    @pl.when(me == LAST)
    def _():
        def scatter(t, carry):
            rows = pl.ds(pl.multiple_of(t * PIECE, PIECE), PIECE)
            remote(cand_l.at[rows], gfull.at[1, rows], ls.at[t], lr, t).start()
            return carry

        lax.fori_loop(0, LAST, scatter, 0)
        gfull[1, pl.ds(LAST * PIECE, PIECE), :] = cand_l[pl.ds(LAST * PIECE, PIECE), :]

    halos = []
    for kv, ref in ((0, k_ref), (1, v_ref)):
        for side, rows, target in (
            (0, pl.ds((QB - 1) * BLOCK, BLOCK), after),
            (1, pl.ds(0, BLOCK), before),
        ):
            copy = remote(
                ref.at[rows], halo.at[side, kv], hs.at[2 * side + kv], hr.at[2 * side + kv], target
            )
            copy.start()
            halos.append(copy)

    ay[0] = cand_o[pl.ds(pl.multiple_of(y * QUART, QUART), QUART), :]
    mine = pl.ds(pl.multiple_of(me * PIECE, PIECE), PIECE)
    quarter = pl.ds(pl.multiple_of(y * QUART, QUART), QUART)
    across, spread, raised = [], [], []
    for number, offsets in enumerate(ROUNDS):
        if number >= 2:
            sent_round(me, payload, recv, ss, rs, ROUNDS[number - 2])
        send_round(me, 1, payload, recv, ss, rs, offsets)
        if number == 2:
            for copy in up:
                copy.wait_recv()
            gq[...] = ay[sel[0]]
        if number == 3:
            for dp in range(1, 16):
                target = plane_target(me, dp)
                rows = pl.ds(pl.multiple_of(lax.rem(target, 16) * PIECE, PIECE), PIECE)
                copy = remote(gq.at[rows], ap.at[dp], ps.at[dp], pr.at[dp], target)
                copy.start()
                across.append(copy)
            ap[0] = gq[pl.ds(pl.multiple_of(plane * PIECE, PIECE), PIECE), :]
        if number == 5:
            for copy in across:
                copy.wait_recv()
            gfull[0, mine, :] = ap[sel[1]]

            @pl.when(me != LAST)
            def _():
                remote(cand_l.at[mine], gfull.at[1, mine], ls.at[0], lr, me).wait_recv()

        if number == 6:
            for dp in range(1, 16):
                copy = remote(
                    gfull.at[:, mine], gfull.at[:, mine], bs.at[dp], br.at[dp], plane_target(me, dp)
                )
                copy.start()
                spread.append(copy)
        if number == 8:
            for copy in spread:
                copy.wait_recv()
            for dy in range(1, 4):
                copy = remote(
                    gfull.at[:, quarter], gfull.at[:, quarter], cs.at[dy], cr.at[dy],
                    lax.rem(y + dy, 4) * 16 + plane,
                )
                copy.start()
                raised.append(copy)
    for offsets in ROUNDS[-2:]:
        sent_round(me, payload, recv, ss, rs, offsets)
    for offsets in ROUNDS:
        arrived_round(me, payload, recv, ss, rs, offsets)
    for copy in up + across + spread:
        copy.wait_send()
    for copy in raised + halos:
        copy.wait()

    @pl.when(me == LAST)
    def _():
        def done(t, carry):
            rows = pl.ds(pl.multiple_of(t * PIECE, PIECE), PIECE)
            remote(cand_l.at[rows], gfull.at[1, rows], ls.at[t], lr, t).wait_send()
            return carry

        lax.fori_loop(0, LAST, done, 0)

    own.wait()


def nt(a, b):
    return lax.dot_general(a, b, (((1,), (1,)), ((), ())), preferred_element_type=F32)


def nn(a, b):
    return lax.dot_general(a, b, (((1,), (0,)), ((), ())), preferred_element_type=F32)


def tn(a, b):
    return lax.dot_general(a, b, (((0,), (0,)), ((), ())), preferred_element_type=F32)


def attend_kernel(
    pick, q_ref, k_ref, v_ref, g_ref, halo_ref, glob_ref, recv,
    out_ref, dq_ref, center_ref, rim_ref, gpart_ref, outgoing,
    rk, rv, tk, tv, bandk, bandv, gk, gv, acck, accv, dsg, pgs, in_sem, out_sem,
):
    me = lax.axis_index("seq")
    h = pl.program_id(0)
    slot = lax.rem(h, 2)
    per_head = QB * RAND

    def load(head, buf):
        for e in range(per_head):
            s = pick[head * per_head + e]
            d, c = lax.div(s, 2), lax.rem(s, 2)
            rows = pl.ds(e * BLOCK, BLOCK)
            pltpu.make_async_copy(recv.at[d, c, 0], rk.at[buf, rows], in_sem.at[buf]).start()
            pltpu.make_async_copy(recv.at[d, c, 1], rv.at[buf, rows], in_sem.at[buf]).start()

    def drain(buf):
        pltpu.make_async_copy(tk.at[buf], tk.at[buf], out_sem.at[buf]).wait()
        pltpu.make_async_copy(tv.at[buf], tv.at[buf], out_sem.at[buf]).wait()

    @pl.when(h == 0)
    def _():
        load(0, 0)

    @pl.when(h + 1 < HEADS_HERE)
    def _():
        load(h + 1, 1 - slot)

    rows_here = QB * BLOCK
    for band, kv, ref in ((bandk, 0, k_ref), (bandv, 1, v_ref)):
        band[0:BLOCK] = halo_ref[0, kv]
        band[BLOCK : BLOCK + rows_here] = ref[...]
        band[BLOCK + rows_here :] = halo_ref[1, kv]
    for g in range(2):
        gk[g * BLOCK : (g + 1) * BLOCK] = glob_ref[g, 0, 0]
        gv[g * BLOCK : (g + 1) * BLOCK] = glob_ref[g, 0, 1]
    acck[...] = jnp.zeros_like(acck)
    accv[...] = jnp.zeros_like(accv)
    pltpu.make_async_copy(rk.at[slot], rk.at[slot], in_sem.at[slot]).wait()
    pltpu.make_async_copy(rv.at[slot], rv.at[slot], in_sem.at[slot]).wait()

    @pl.when(h >= 2)
    def _():
        drain(slot)

    span = 3 * BLOCK
    col = lax.broadcasted_iota(jnp.int32, (BLOCK, span), 1)
    for i in range(QB):
        mine = slice(i * BLOCK, (i + 1) * BLOCK)
        q = q_ref[mine, :]
        g = g_ref[mine, :]
        wk, wv = bandk[i * BLOCK : i * BLOCK + span], bandv[i * BLOCK : i * BLOCK + span]
        ek, ev = rk[slot, i * span : (i + 1) * span], rv[slot, i * span : (i + 1) * span]
        sw = nt(q, wk) * SCALE
        if i == 0:
            sw = jnp.where((col < BLOCK) & (me == 0), MASKED, sw)
        if i == QB - 1:
            sw = jnp.where((col >= 2 * BLOCK) & (me == LAST), MASKED, sw)
        sr = nt(q, ek) * SCALE
        sg = nt(q, gk[...]) * SCALE
        peak = jnp.maximum(
            jnp.maximum(jnp.max(sw, axis=1, keepdims=True), jnp.max(sr, axis=1, keepdims=True)),
            jnp.max(sg, axis=1, keepdims=True),
        )
        sw, sr, sg = jnp.exp(sw - peak), jnp.exp(sr - peak), jnp.exp(sg - peak)
        total = (
            jnp.sum(sw, axis=1, keepdims=True)
            + jnp.sum(sr, axis=1, keepdims=True)
            + jnp.sum(sg, axis=1, keepdims=True)
        )
        inverse = 1.0 / total
        sw, sr, sg = sw * inverse, sr * inverse, sg * inverse
        pw, pr, pg = sw.astype(BF), sr.astype(BF), sg.astype(BF)
        out = (nn(pw, wv) + nn(pr, ev) + nn(pg, gv[...])).astype(BF)
        out_ref[mine, :] = out
        delta = jnp.sum(g.astype(F32) * out.astype(F32), axis=1, keepdims=True)
        dw = (sw * (nt(g, wv) - delta)).astype(BF)
        dr = (sr * (nt(g, ev) - delta)).astype(BF)
        dg = (sg * (nt(g, gv[...]) - delta)).astype(BF)
        dq_ref[mine, :] = ((nn(dw, wk) + nn(dr, ek) + nn(dg, gk[...])) * SCALE).astype(BF)
        acck[i * BLOCK : i * BLOCK + span] += tn(dw, q)
        accv[i * BLOCK : i * BLOCK + span] += tn(pw, g)
        tk[slot, i * span : (i + 1) * span] = (tn(dr, q) * SCALE).astype(BF)
        tv[slot, i * span : (i + 1) * span] = tn(pr, g).astype(BF)
        dsg[mine, :] = dg
        pgs[mine, :] = pg
    gdk = tn(dsg[...], q_ref[...]) * SCALE
    gdv = tn(pgs[...], g_ref[...])
    for g in range(2):
        gpart_ref[g, 0, 0] = gdk[g * BLOCK : (g + 1) * BLOCK].astype(BF)
        gpart_ref[g, 0, 1] = gdv[g * BLOCK : (g + 1) * BLOCK].astype(BF)
    center_ref[0] = acck[BLOCK : BLOCK + rows_here] * SCALE
    center_ref[1] = accv[BLOCK : BLOCK + rows_here]
    rim_ref[0, 0] = (acck[0:BLOCK] * SCALE).astype(BF)
    rim_ref[0, 1] = accv[0:BLOCK].astype(BF)
    rim_ref[1, 0] = (acck[BLOCK + rows_here :] * SCALE).astype(BF)
    rim_ref[1, 1] = accv[BLOCK + rows_here :].astype(BF)
    for e in range(per_head):
        s = pick[h * per_head + e]
        d, c = lax.div(s, 2), lax.rem(s, 2)
        rows = pl.ds(e * BLOCK, BLOCK)
        pltpu.make_async_copy(tk.at[slot, rows], outgoing.at[d, c, 0], out_sem.at[slot]).start()
        pltpu.make_async_copy(tv.at[slot, rows], outgoing.at[d, c, 1], out_sem.at[slot]).start()

    @pl.when(h == HEADS_HERE - 1)
    def _():
        drain(1 - slot)
        drain(slot)


def return_kernel(
    outgoing, rim, gpart, returned, rim_back, gtot, glast,
    ry, g1, rp, g2, ss, rs, hs, hr, ys, yr, ps, pr, ls, lr, bs, br, cs, cr, own_sem,
):
    me = lax.axis_index("seq")
    y = lax.div(me, 16)
    plane = lax.rem(me, 16)
    enter(me)
    after = lax.rem(me + 1, SHARDS)
    before = lax.rem(me + SHARDS - 1, SHARDS)
    own = pltpu.make_async_copy(outgoing.at[0], returned.at[0], own_sem)
    own.start()
    up = []
    for dy in range(1, 4):
        ty = lax.rem(y + dy, 4)
        copy = remote(
            gpart.at[:, pl.ds(pl.multiple_of(ty * QUART, QUART), QUART)],
            ry.at[dy - 1], ys.at[dy], yr.at[dy], ty * 16 + plane,
        )
        copy.start()
        up.append(copy)
    halos = []
    for kv in range(2):
        for side, target in ((0, before), (1, after)):
            copy = remote(
                rim.at[side, kv], rim_back.at[1 - side, kv],
                hs.at[2 * side + kv], hr.at[2 * side + kv], target,
            )
            copy.start()
            halos.append(copy)
    mine = pl.ds(pl.multiple_of(me * PIECE, PIECE), PIECE)
    quarter = pl.ds(pl.multiple_of(y * QUART, QUART), QUART)
    part = pl.ds(pl.multiple_of(plane * PIECE, PIECE), PIECE)
    across, spread, raised = [], [], []
    for number, offsets in enumerate(ROUNDS):
        if number >= 2:
            sent_round(me, outgoing, returned, ss, rs, ROUNDS[number - 2])
        send_round(me, -1, outgoing, returned, ss, rs, offsets)
        if number == 3:
            for copy in up:
                copy.wait_recv()
            for g in range(2):
                g1[g] = (
                    gpart[g, quarter, :].astype(F32)
                    + ry[0, g].astype(F32)
                    + ry[1, g].astype(F32)
                    + ry[2, g].astype(F32)
                ).astype(BF)
        if number == 4:
            for dp in range(1, 16):
                target = plane_target(me, dp)
                rows = pl.ds(pl.multiple_of(lax.rem(target, 16) * PIECE, PIECE), PIECE)
                copy = remote(g1.at[:, rows], rp.at[dp], ps.at[dp], pr.at[dp], target)
                copy.start()
                across.append(copy)
        if number == 6:
            for copy in across:
                copy.wait_recv()
            total = g1[:, part, :].astype(F32)
            for dp in range(1, 16):
                total = total + rp[dp].astype(F32)
            g2[...] = total.astype(BF)
            gtot[mine, :] = total[0].astype(BF)
        if number == 7:

            @pl.when(me != LAST)
            def _():
                remote(g2.at[1], glast.at[mine], ls, lr.at[me], LAST).start()

            @pl.when(me == LAST)
            def _():
                glast[mine, :] = g2[1]

            for dp in range(1, 16):
                copy = remote(
                    gtot.at[mine], gtot.at[mine], bs.at[dp], br.at[dp], plane_target(me, dp)
                )
                copy.start()
                spread.append(copy)
        if number == 9:
            for copy in spread:
                copy.wait_recv()
            for dy in range(1, 4):
                copy = remote(
                    gtot.at[quarter], gtot.at[quarter], cs.at[dy], cr.at[dy],
                    lax.rem(y + dy, 4) * 16 + plane,
                )
                copy.start()
                raised.append(copy)
    for offsets in ROUNDS[-2:]:
        sent_round(me, outgoing, returned, ss, rs, offsets)
    for offsets in ROUNDS:
        arrived_round(me, outgoing, returned, ss, rs, offsets)
    for copy in up + across + spread:
        copy.wait_send()
    for copy in raised + halos:
        copy.wait()

    @pl.when(me != LAST)
    def _():
        remote(g2.at[1], glast.at[mine], ls, lr.at[me], LAST).wait_send()

    @pl.when(me == LAST)
    def _():
        def done(t, carry):
            rows = pl.ds(pl.multiple_of(t * PIECE, PIECE), PIECE)
            remote(g2.at[1], glast.at[rows], ls, lr.at[t], t).wait_recv()
            return carry

        lax.fori_loop(0, LAST, done, 0)

    own.wait()


CHUNK = 4


def collect_kernel(
    cmin, cmax, misc, center, rim, gtot, glast, returned, dk_ref, dv_ref, buf, acc, sem, csem
):
    me = lax.axis_index("seq")
    steps = SHARDS // CHUNK

    def fetch(step, slot):
        return pltpu.make_async_copy(
            returned.at[pl.ds(step * CHUNK, CHUNK)], buf.at[slot], sem.at[slot]
        )

    whole = pltpu.make_async_copy(center, acc, csem)
    whole.start()
    fetch(0, 0).start()
    whole.wait()
    for kv in range(2):
        acc[kv, 0:BLOCK, :] += rim[0, kv].astype(F32)
        acc[kv, (QB - 1) * BLOCK :, :] += rim[1, kv].astype(F32)

    def add_glob(blk, ref):
        rows = pl.ds(pl.multiple_of(blk * BLOCK, BLOCK), BLOCK)
        for h in range(HEADS_HERE):
            for kv in range(2):
                src = ref[pl.ds((2 * h + kv) * BLOCK, BLOCK), :]
                acc[kv, rows, pl.ds(h * DH, DH)] += src.astype(F32)

    @pl.when(me == LAST)
    def _():
        add_glob(QB - 1, glast)

    @pl.when(me == misc[1])
    def _():
        add_glob(misc[0], gtot)

    def add(code, slot, place, c):
        head = lax.div(code, 4 * QB * RAND)
        blk = lax.rem(code, 4)
        rows = pl.ds(pl.multiple_of(blk * BLOCK, BLOCK), BLOCK)
        cols = pl.ds(pl.multiple_of(head * DH, DH), DH)
        for kv in range(2):
            acc[kv, rows, cols] += buf[slot, place, c, kv].astype(F32)

    def step_body(step, carry):
        slot = lax.rem(step, 2)

        @pl.when(step + 1 < steps)
        def _():
            fetch(step + 1, 1 - slot).start()

        fetch(step, slot).wait()
        for place in range(CHUNK):
            t = moved(me, step * CHUNK + place)
            low, high = cmin[t], cmax[t]

            @pl.when(low < NONE)
            def _():
                add(low, slot, place, 0)

            @pl.when(high > low)
            def _():
                add(high, slot, place, 1)

        return carry

    lax.fori_loop(0, steps, step_body, 0)
    dk_ref[...] = acc[0].astype(BF)
    dv_ref[...] = acc[1].astype(BF)


def smem():
    return pl.BlockSpec(memory_space=pltpu.SMEM)


def vmem():
    return pl.BlockSpec(memory_space=pltpu.VMEM)


def hbm():
    return pl.BlockSpec(memory_space=ANY)


def dma(*shape):
    return pltpu.SemaphoreType.DMA(shape)


def body(queries, keys, values, out_grad, rand_ids, glob_ids):
    place = lax.axis_index("seq")
    group = lax.axis_index("head")
    shape = jax.ShapeDtypeStruct
    ids = lax.dynamic_slice_in_dim(rand_ids, group * HEADS_HERE, HEADS_HERE, 0)
    ids = ids.reshape(HEADS_HERE, SHARDS, QB * RAND)
    number = (
        jnp.arange(HEADS_HERE, dtype=jnp.int32)[:, None, None] * (QB * RAND)
        + jnp.arange(QB * RAND, dtype=jnp.int32)[None, None, :]
    )
    code = number * 4 + lax.rem(ids, 4)
    hit = lax.div(ids, 4) == place
    cmin = jnp.min(jnp.where(hit, code, NONE), axis=(0, 2))
    cmax = jnp.max(jnp.where(hit, code, -1), axis=(0, 2))
    own = lax.dynamic_index_in_dim(ids, place, 1, False).reshape(ENTRIES)
    src = lax.div(own, 4)
    order = jnp.arange(ENTRIES, dtype=jnp.int32)
    again = jnp.any((src[:, None] == src[None, :]) & (order[None, :] < order[:, None]), axis=1)

    def part(value, step):
        return lax.rem(lax.div(value, step), 4)

    def away(a, b):
        return sum(lax.rem(part(a, s) - part(b, s) + 4, 4) * s for s in (16, 4, 1))

    pick = away(place, src) * 2 + again.astype(jnp.int32)
    other = glob_ids[0] + glob_ids[1] - (SHARDS * QB - 1)
    root = lax.div(other, QB)
    misc = jnp.stack([lax.rem(other, QB), root])
    sel = jnp.stack([lax.div(away(place, root), 16), lax.rem(away(place, root), 16)])
    slots = shape((SHARDS, 2, 2, BLOCK, DH), BF)
    width = HEADS_HERE * DH
    rows_here = QB * BLOCK

    payload, cand_o, cand_l = pl.pallas_call(
        prep_kernel,
        out_shape=(slots, shape((GROWS, DH), BF), shape((GROWS, DH), BF)),
        in_specs=[smem(), smem(), smem(), vmem(), vmem()],
        out_specs=(hbm(), hbm(), hbm()),
        scratch_shapes=[pltpu.SemaphoreType.DMA, dma(2)],
        name="prep",
    )(cmin, cmax, misc, keys, values)

    recv, halo, gfull = pl.pallas_call(
        fetch_kernel,
        out_shape=(slots, shape((2, 2, BLOCK, width), BF), shape((2, GROWS, DH), BF)),
        in_specs=[smem(), hbm(), hbm(), hbm(), vmem(), vmem()],
        out_specs=(hbm(), hbm(), vmem()),
        scratch_shapes=[
            pltpu.VMEM((4, QUART, DH), BF),
            pltpu.VMEM((QUART, DH), BF),
            pltpu.VMEM((16, PIECE, DH), BF),
            dma(SHARDS), dma(SHARDS), dma(4), dma(4), dma(4), dma(4), dma(16), dma(16),
            dma(SHARDS), pltpu.SemaphoreType.DMA, dma(16), dma(16), dma(4), dma(4),
            pltpu.SemaphoreType.DMA,
        ],
        compiler_params=pltpu.CompilerParams(collective_id=0, has_side_effects=True),
        name="fetch",
    )(sel, payload, keys, values, cand_o, cand_l)

    span = 3 * BLOCK
    head_block = pl.BlockSpec((rows_here, DH), lambda h, *_: (0, h))
    side_block = pl.BlockSpec((2, 2, BLOCK, DH), lambda h, *_: (0, 0, 0, h))
    glob_block = pl.BlockSpec((2, 1, 2, BLOCK, DH), lambda h, *_: (0, h, 0, 0, 0))
    full = QB * span
    out, dq, center, rim, gpart, outgoing = pl.pallas_call(
        attend_kernel,
        out_shape=(
            shape((rows_here, width), BF),
            shape((rows_here, width), BF),
            shape((2, rows_here, width), F32),
            shape((2, 2, BLOCK, width), BF),
            shape((2, HEADS_HERE, 2, BLOCK, DH), BF),
            slots,
        ),
        grid_spec=pltpu.PrefetchScalarGridSpec(
            num_scalar_prefetch=1,
            grid=(HEADS_HERE,),
            in_specs=[head_block] * 4 + [side_block, glob_block, hbm()],
            out_specs=[
                head_block,
                head_block,
                pl.BlockSpec((2, rows_here, DH), lambda h, *_: (0, 0, h)),
                side_block,
                glob_block,
                hbm(),
            ],
            scratch_shapes=[pltpu.VMEM((2, full, DH), BF)] * 4
            + [pltpu.VMEM((rows_here + 2 * BLOCK, DH), BF)] * 2
            + [pltpu.VMEM((2 * BLOCK, DH), BF)] * 2
            + [pltpu.VMEM((rows_here + 2 * BLOCK, DH), F32)] * 2
            + [pltpu.VMEM((rows_here, 2 * BLOCK), BF)] * 2
            + [dma(2), dma(2)],
        ),
        name="attend",
    )(
        pick, queries, keys, values, out_grad, halo,
        gfull.reshape(2, HEADS_HERE, 2, BLOCK, DH), recv,
    )

    returned, rim_back, gtot, glast = pl.pallas_call(
        return_kernel,
        out_shape=(
            slots,
            shape((2, 2, BLOCK, width), BF),
            shape((GROWS, DH), BF),
            shape((GROWS, DH), BF),
        ),
        in_specs=[hbm(), hbm(), vmem()],
        out_specs=(hbm(), hbm(), vmem(), vmem()),
        scratch_shapes=[
            pltpu.VMEM((3, 2, QUART, DH), BF),
            pltpu.VMEM((2, QUART, DH), BF),
            pltpu.VMEM((16, 2, PIECE, DH), BF),
            pltpu.VMEM((2, PIECE, DH), BF),
            dma(SHARDS), dma(SHARDS), dma(4), dma(4), dma(4), dma(4), dma(16), dma(16),
            pltpu.SemaphoreType.DMA, dma(SHARDS), dma(16), dma(16), dma(4), dma(4),
            pltpu.SemaphoreType.DMA,
        ],
        compiler_params=pltpu.CompilerParams(collective_id=1, has_side_effects=True),
        name="return",
    )(outgoing, rim, gpart.reshape(2, GROWS, DH))

    dk, dv = pl.pallas_call(
        collect_kernel,
        out_shape=(shape((rows_here, width), BF), shape((rows_here, width), BF)),
        in_specs=[smem(), smem(), smem(), hbm(), vmem(), vmem(), vmem(), hbm()],
        out_specs=(vmem(), vmem()),
        scratch_shapes=[
            pltpu.VMEM((2, CHUNK, 2, 2, BLOCK, DH), BF),
            pltpu.VMEM((2, rows_here, width), F32),
            dma(2),
            pltpu.SemaphoreType.DMA,
        ],
        name="collect",
    )(cmin, cmax, misc, center, rim_back, gtot, glast, returned)
    return out, dq, dk, dv


def solution(mesh):
    rows = P("seq", "head")
    return jax.shard_map(
        body,
        mesh=mesh,
        in_specs=(rows, rows, rows, rows, P(), P()),
        out_specs=(rows, rows, rows, rows),
        check_vma=False,
    )
```

time: 760 us -> 399 us (0.53)
  the two profiles are of different devices: /device:TPU:54 before, /device:TPU:34 now
where the time goes in v1:
time: 399 us; the launch traced here: 394 us
  Pallas kernels  377 us (94%)
  other arithmetic  12.5 us (3%)
    pallas_call x1, Pallas kernels, body(): pl.pallas_call(fetch_kernel, out_shape=(slots, shape((2, 2, BLOCK, width)...  160 us
    pallas_call x1, Pallas kernels, body(): pl.pallas_call(return_kernel, out_shape=(slots, shape((2, 2, BLOCK, width...  159 us
    pallas_call x1, Pallas kernels, body(): pl.pallas_call(attend_kernel, out_shape=(shape((rows_here, width), BF), s...  37.2 us
    pallas_call x1, Pallas kernels, body(): pl.pallas_call(collect_kernel, out_shape=(shape((rows_here, width), BF),...  15.8 us
    reduce_max x2, other arithmetic, body(): cmax = jnp.max(jnp.where(hit, code, -1), axis=(0, 2))  9.81 us

profile of v1, /device:TPU:34, one launch (start us, length us, event | category | flops | bytes accessed | tf_op | source)
XLA Modules:
  0.0 394.2 jit_solution(1378731000029887480)
XLA Ops:
  0.6 0.0 copy-start
  0.7 1.3 fusion.15
  3.4 0.6 pad_add_fusion.sel
  4.0 0.6 pad_add_fusion.1.misc
  4.6 0.0 copy-done
  4.6 0.2 copy.14
  4.9 0.2 add.99
  5.1 9.2 %select_reduce_fusion = (s32[256]{0:T(256)S(1)}, s32[256]{0:T(256)S(1)}) fusion(s32[8,256,3]{0,2,1:T(4,128)S(1)} %add.99, s32[8,256,3]{0,2,1:T(4,128)S(1)} %copy.14, s32[]{:T(128)S(6)} %axis_index.23), kind=kLoop, calls=%fused_computation.5 | loop fusion | flops 91648 | bytes 51204 | tf_op jit(solution)/shard_map/reduce_max | solution.py:604
  14.2 0.2 reshape.93
  14.4 0.1 copy.13
  14.5 0.1 reshape.94
  14.6 0.2 fusion.3
  14.8 0.6 convert_add_fusion.pick
  15.4 0.1 reduce_max.14
  15.5 0.7 reduce_max.18.cmax
  16.2 0.1 reduce_min.14
  16.3 0.6 reduce_min.18.cmin
  16.9 5.0 %prep.1 = (bf16[64,2,2,128,128]{4,3,2,1,0:T(8,128)(2,1)}, bf16[2048,128]{1,0:T(8,128)(2,1)}, bf16[2048,128]{1,0:T(8,128)(2,1)}) custom-call(s32[64]{0:T(128)} %reduce_min.18.cmin, s32[64]{0:T(128)} %reduce_max.18.cmax, s32[2]{0:T(128)} %pad_add_fusion.1.misc, bf16[512,1024]{1,0:T(8,128)(2,1)} %k_ref.5, bf16[512,1024]{1,0:T(8,128)(2,1)} %v_ref.5), custom_call_target="tpu_custom_call" | custom-call | tf_op jit(solution)/shard_map/prep/pallas_call | solution.py:625
  21.9 160.0 %fetch.1 = (bf16[64,2,2,128,128]{4,3,2,1,0:T(8,128)(2,1)}, bf16[2,2,128,1024]{3,2,1,0:T(8,128)(2,1)}, bf16[2,2048,128]{2,1,0:T(8,128)(2,1)}) custom-call(s32[2]{0:T(128)} %pad_add_fusion.sel, bf16[64,2,2,128,128]{4,3,2,1,0:T(8,128)(2,1)} %get-tuple-element.22.payload, bf16[512,1024]{1,0:T(8,128)(2,1)} %k_ref.5, bf16[512,1024]{1,0:T(8,128)(2,1)} %v_ref.5, ...), custom_call_target="tpu_custom_call" | custom-call | tf_op jit(solution)/shard_map/fetch/pallas_call | solution.py:634
  181.9 37.2 %attend.1 = (bf16[512,1024]{1,0:T(8,128)(2,1)}, bf16[512,1024]{1,0:T(8,128)(2,1)}, f32[2,512,1024]{2,1,0:T(8,128)}, bf16[2,2,128,1024]{3,2,1,0:T(8,128)(2,1)}, b...) custom-call(s32[96]{0:T(128)} %convert_add_fusion.pick, bf16[512,1024]{1,0:T(8,128)(2,1)} %q_ref.1, ...), custom_call_target="tpu_custom_call" | custom-call | tf_op jit(solution)/shard_map/attend/pallas_call | solution.py:656
  219.2 159.1 %return.1 = (bf16[64,2,2,128,128]{4,3,2,1,0:T(8,128)(2,1)}, bf16[2,2,128,1024]{3,2,1,0:T(8,128)(2,1)}, bf16[2048,128]{1,0:T(8,128)(2,1)}, bf16[2048,128]{1,0:T(8,128)(2,1)}) custom-call(bf16[64,2,2,128,128]{4,3,2,1,0:T(8,128)(2,1)} %get-tuple-element.31.outgoing, bf16[2,2,128,1024]{3,2,1,0:T(8,128)(2,1)} %get-tuple-element.32.rim, bf16[2,2048,128]{2,1,0:T(8,128)(2,1)} %bitcast.14), custom_call_target="tpu_custom_call" | custom-call | tf_op jit(solution)/shard_map/return/pallas_call | solution.py:691
  378.2 15.8 %collect.1 = (bf16[512,1024]{1,0:T(8,128)(2,1)}, bf16[512,1024]{1,0:T(8,128)(2,1)}) custom-call(s32[64]{0:T(128)} %reduce_min.18.cmin, s32[64]{0:T(128)} %reduce_max.18.cmax, s32[2]{0:T(128)} %pad_add_fusion.1.misc, f32[2,512,1024]{2,1,0:T(8,128)} %get-tuple-element.30.center, bf16[2,2,128,1024]{3,2,1,0:T(8,128)(2,1)} %get-tuple-element.34.rim, ...), custom_call_target="tpu_custom_call" | custom-call | tf_op jit(solution)/shard_map/collect/pallas_call | solution.py:714
  (6 shorter events, 0.1 us)
Async XLA Ops:
  0.6 4.0 %copy-start = (s32[16,256,3]{1,0,2:T(8,128)S(1)}, s32[16,256,3]{1,0,2:T(8,128)}, u32[]{:S(2)}) copy-start(s32[16,256,3]{1,0,2:T(8,128)} %param.10) | copy-start | bytes 147460

commit v2 on v1

v2 whole, which is shorter than its diff:
```python
import functools
import math

import jax
import jax.numpy as jnp
from jax import lax
from jax.experimental import pallas as pl
from jax.experimental.pallas import tpu as pltpu
from jax.sharding import PartitionSpec as P

BLOCK = 128
DH = 128
RAND = 3
HEADS_HERE = 8
QB = 4
SHARDS = 64
ENTRIES = HEADS_HERE * QB * RAND
NONE = 1 << 20
DEPTH = 6
FETCH_AT = (1, 2, 3, 4, 8)
FAR_AT = (1, 2, 3, 4, 5, 6, 7, 8)
RETURN_AT = (3, 4, 5, 6, 8)
LAST = SHARDS - 1
GROWS = HEADS_HERE * 2 * BLOCK
PIECE = GROWS // SHARDS
QUART = GROWS // 4
SCALE = 1.0 / math.sqrt(DH)
MASKED = -1e30
MESH = pl.DeviceIdType.MESH
ANY = pl.ANY
BF = jnp.bfloat16
F32 = jnp.float32


def orbits():
    def key(d):
        return (d // 16, (d // 4) % 4, d % 4)

    def hops(d):
        return sum(min(v, 4 - v) for v in key(d))

    seen, rounds = set(), []
    for d in sorted(range(1, SHARDS), key=lambda d: (hops(d), d)):
        if d in seen:
            continue
        orbit = []
        for turn in range(3):
            k = key(d)[turn:] + key(d)[:turn]
            for sign in (1, -1):
                a, b, c = ((sign * v) % 4 for v in k)
                if a * 16 + b * 4 + c not in orbit:
                    orbit.append(a * 16 + b * 4 + c)
        seen.update(orbit)
        rounds.append(orbit)
    return rounds


ROUNDS = orbits()


def moved(me, d, sign=1):
    y, z, x = lax.div(me, 16), lax.rem(lax.div(me, 4), 4), lax.rem(me, 4)
    dy, dz, dx = lax.div(d, 16), lax.rem(lax.div(d, 4), 4), lax.rem(d, 4)
    if sign < 0:
        dy, dz, dx = 4 - dy, 4 - dz, 4 - dx
    return lax.rem(y + dy, 4) * 16 + lax.rem(z + dz, 4) * 4 + lax.rem(x + dx, 4)


def shifted(me, d, sign=1):
    dy, dz, dx = d // 16, (d // 4) % 4, d % 4
    if sign < 0:
        dy, dz, dx = 4 - dy, 4 - dz, 4 - dx
    y, z, x = lax.div(me, 16), lax.rem(lax.div(me, 4), 4), lax.rem(me, 4)
    return lax.rem(y + dy, 4) * 16 + lax.rem(z + dz, 4) * 4 + lax.rem(x + dx, 4)


def remote(src, dst, send, recv, target):
    return pltpu.make_async_remote_copy(
        src_ref=src,
        dst_ref=dst,
        send_sem=send,
        recv_sem=recv,
        device_id={"seq": target},
        device_id_type=MESH,
    )


def enter(me):
    barrier = pltpu.get_barrier_semaphore()

    def greet(d, carry):
        pl.semaphore_signal(
            barrier, inc=1, device_id={"seq": moved(me, d)}, device_id_type=MESH
        )
        return carry

    lax.fori_loop(1, SHARDS, greet, 0)
    pl.semaphore_wait(barrier, SHARDS - 1)


def prep_kernel(
    glob, own_ids, ids, k_ref, v_ref, payload, cand_o, cand_l, pick, codes, count, table, sem,
    gsem, tsem,
):
    me = lax.axis_index("seq")
    entry = lax.broadcasted_iota(jnp.int32, (ENTRIES, SHARDS), 0)
    code = entry * 4 + (ids[...] & 3)
    hit = (ids[...] >> 2) == me
    codes[0:1, :] = jnp.min(jnp.where(hit, code, NONE), axis=0, keepdims=True)
    codes[1:2, :] = jnp.max(jnp.where(hit, code, -1), axis=0, keepdims=True)
    to_scalar = pltpu.make_async_copy(codes, table, tsem)
    to_scalar.start()
    other = glob[0] + glob[1] - (SHARDS * QB - 1)
    rows_o = pl.ds(pl.multiple_of(lax.rem(other, QB) * BLOCK, BLOCK), BLOCK)
    rows_l = pl.ds((QB - 1) * BLOCK, BLOCK)
    for h in range(HEADS_HERE):
        cols = pl.ds(h * DH, DH)
        for kv, ref in ((0, k_ref), (1, v_ref)):
            dst = pl.ds((2 * h + kv) * BLOCK, BLOCK)
            pltpu.make_async_copy(ref.at[rows_o, cols], cand_o.at[dst], gsem.at[0]).start()
            pltpu.make_async_copy(ref.at[rows_l, cols], cand_l.at[dst], gsem.at[1]).start()
    to_scalar.wait()

    def put(d, carry):
        t = moved(me, d)
        low = table[0, t]
        high = table[1, t]
        count[t] = 0
        for c, code in ((0, jnp.where(low < NONE, low, 0)), (1, jnp.maximum(high, 0))):
            head = lax.div(code, 4 * QB * RAND)
            blk = lax.rem(code, 4)
            rows = pl.ds(pl.multiple_of(blk * BLOCK, BLOCK), BLOCK)
            cols = pl.ds(pl.multiple_of(head * DH, DH), DH)
            pltpu.make_async_copy(k_ref.at[rows, cols], payload.at[d, c, 0], sem).start()
            pltpu.make_async_copy(v_ref.at[rows, cols], payload.at[d, c, 1], sem).start()
        return carry

    lax.fori_loop(0, SHARDS, put, 0)

    def choose(e, carry):
        src = lax.div(own_ids[e], 4)
        seen = count[src]
        count[src] = seen + 1
        away = 0
        for axis in "yzx":
            gap = lax.rem(place_of(me, axis) + 4 - place_of(src, axis), 4)
            away = away + gap * STEP[axis]
        pick[e] = away * 2 + jnp.minimum(seen, 1)
        return carry

    lax.fori_loop(0, ENTRIES, choose, 0)
    pltpu.make_async_copy(cand_o, cand_o, gsem.at[0]).wait()
    pltpu.make_async_copy(cand_l, cand_l, gsem.at[1]).wait()
    pltpu.make_async_copy(payload, payload, sem).wait()


def send_round(me, sign, src, dst, ss, rs, offsets):
    def piece(i, carry):
        c, kv = lax.div(i, 2), lax.rem(i, 2)
        for d in offsets:
            remote(
                src.at[d, c, kv], dst.at[d, c, kv], ss.at[d], rs.at[d], shifted(me, d, sign)
            ).start()
        return carry

    lax.fori_loop(0, 4, piece, 0)


def sent_round(me, src, dst, ss, rs, offsets):
    for d in offsets:
        remote(src.at[d], dst.at[d], ss.at[d], rs.at[d], me).wait_send()


def arrived_round(me, src, dst, ss, rs, offsets):
    for d in offsets:
        remote(src.at[d], dst.at[d], ss.at[d], rs.at[d], me).wait_recv()


STEP = {"y": 16, "z": 4, "x": 1}


def place_of(me, axis):
    return lax.rem(lax.div(me, STEP[axis]), 4)


def along(me, axis, delta):
    here = place_of(me, axis)
    there = lax.rem(here + delta, 4)
    return there, me + (there - here) * STEP[axis]


def order_of(me, order):
    first, second, third = (place_of(me, axis) for axis in order)
    return first * 16 + second * 4 + third


def chunks(rows):
    return [(r, min(BLOCK, rows)) for r in range(0, rows, BLOCK)]


def scatter_line(me, axis, src, dst, rows, send, recv, base, parts=None):
    for start, size in chunks(rows):
        if parts is not None and start // BLOCK not in parts:
            continue
        for delta in (1, 3, 2):
            there, target = along(me, axis, delta)
            remote(
                src.at[pl.ds(pl.multiple_of(there * rows + start, PIECE), size)],
                dst.at[delta, pl.ds(start, size)],
                send.at[base + delta], recv.at[base + delta], target,
            ).start()


def line_waits(me, ref, send, recv, base):
    return [
        remote(ref.at[delta], ref.at[delta], send.at[base + delta], recv.at[base + delta], me)
        for delta in range(1, 4)
    ]


def share_line(me, axis, full, first, rows, send, recv, base, parts=None):
    for start, size in chunks(rows):
        if parts is not None and start // BLOCK not in parts:
            continue
        for delta in (1, 3, 2):
            target = along(me, axis, delta)[1]
            ref = full.at[pl.ds(pl.multiple_of(first + start, PIECE), size)]
            remote(ref, ref, send.at[base + delta], recv.at[base + delta], target).start()


def share_waits(me, full, rows, send, recv, base):
    ref = full.at[pl.ds(0, rows)]
    return [
        remote(ref, ref, send.at[base + delta], recv.at[base + delta], me) for delta in range(1, 4)
    ]


def spread_order(order):
    return (order[2], PIECE), (order[1], 4 * PIECE), (order[0], QUART)


def first_row(me, order, rows):
    return pl.multiple_of(lax.div(order_of(me, order) * PIECE, rows) * rows, PIECE)


def fetch_kernel(
    glob, payload, k_ref, v_ref, cand_o, cand_l, recv, halo, gother, glast,
    ay, az, ax, gy, gz, ss, rs, hs, hr, us, ur, ls, lr, bs, br, own_sem,
):
    me = lax.axis_index("seq")
    enter(me)
    after = lax.rem(me + 1, SHARDS)
    before = lax.rem(me + SHARDS - 1, SHARDS)
    root = lax.div(glob[0] + glob[1] - (SHARDS * QB - 1), QB)

    def offset_of(axis):
        return lax.rem(place_of(me, axis) + 4 - place_of(root, axis), 4)

    own = pltpu.make_async_copy(payload.at[0], recv.at[0], own_sem)
    own.start()
    orders = ("yzx", "zyx")
    fulls = (gother, glast)
    mine = [pl.ds(first_row(me, order, PIECE), PIECE) for order in orders]

    @pl.when(me == LAST)
    def _():
        def scatter(t, carry):
            rows = pl.ds(first_row(t, "zyx", PIECE), PIECE)
            remote(cand_l.at[rows], glast.at[rows], ls.at[t], lr, t).start()
            return carry

        lax.fori_loop(0, LAST, scatter, 0)
        glast[mine[1], :] = cand_l[mine[1], :]

    def edge(part, far):
        for side, first, target, x in ((0, (QB - 1) * BLOCK, after, 3), (1, 0, before, 0)):

            @pl.when((place_of(me, "x") == x) == far)
            def _():
                for kv, ref in ((0, k_ref), (1, v_ref)):
                    remote(
                        ref.at[pl.ds(first + part * 16, 16)],
                        halo.at[side, kv, pl.ds(part * 16, 16)],
                        hs.at[2 * side + kv], hr.at[2 * side + kv], target,
                    ).start()

    halos = [
        remote(halo.at[n // 2, n % 2], halo.at[n // 2, n % 2], hs.at[n], hr.at[n], me)
        for n in range(4)
    ]
    ay[0] = cand_o[pl.ds(pl.multiple_of(place_of(me, "y") * QUART, QUART), QUART), :]
    up = [line_waits(me, ref, us, ur, 4 * n) for n, ref in enumerate((ay, az, ax))]
    down = [
        [
            share_waits(me, fulls[g], rows, bs, br, 12 * g + 4 * level)
            for level, (axis, rows) in enumerate(spread_order(orders[g]))
        ]
        for g in range(2)
    ]

    def share(g, level, parts=None):
        axis, rows = spread_order(orders[g])[level]
        share_line(
            me, axis, fulls[g], first_row(me, orders[g], rows), rows, bs, br, 12 * g + 4 * level,
            parts,
        )

    for part in range(4):
        scatter_line(me, "y", cand_o, ay, QUART, us, ur, 0, (part,))
        edge(part, False)
    later = []
    for number, offsets in enumerate(ROUNDS):
        if number >= DEPTH:
            sent_round(me, payload, recv, ss, rs, ROUNDS[number - DEPTH])
        for step in later:
            step()
        later = []
        send_round(me, 1, payload, recv, ss, rs, offsets)
        if number in FAR_AT:
            edge(FAR_AT.index(number), True)
        if number == FETCH_AT[0]:
            for copy in up[0]:
                copy.wait_recv()
            gy[...] = ay[offset_of("y")]
            later.append(lambda: scatter_line(me, "z", gy, az, 4 * PIECE, us, ur, 4))
            rows = pl.ds(pl.multiple_of(place_of(me, "z") * 4 * PIECE, 4 * PIECE), 4 * PIECE)
            az[0] = gy[rows, :]

            @pl.when(me != LAST)
            def _():
                remote(cand_l.at[mine[1]], glast.at[mine[1]], ls.at[0], lr, me).wait_recv()

            later.append(lambda: share(1, 0))
        if number == FETCH_AT[1]:
            for copy in up[1]:
                copy.wait_recv()
            gz[...] = az[offset_of("z")]
            later.append(lambda: scatter_line(me, "x", gz, ax, PIECE, us, ur, 8))
            ax[0] = gz[pl.ds(pl.multiple_of(place_of(me, "x") * PIECE, PIECE), PIECE), :]
            for copy in down[1][0]:
                copy.wait_recv()
            share(1, 1)
        if number == FETCH_AT[2]:
            for copy in up[2]:
                copy.wait_recv()
            gother[mine[0], :] = ax[offset_of("x")]
            later.append(lambda: share(0, 0))
            for copy in down[1][1]:
                copy.wait_recv()
        if number == FETCH_AT[3]:
            for copy in down[0][0]:
                copy.wait_recv()
            share(0, 1)
        if number == FETCH_AT[4]:
            for copy in down[0][1]:
                copy.wait_recv()
        if FETCH_AT[4] <= number < FETCH_AT[4] + 4:
            part = number - FETCH_AT[4]
            share(0, 2, (part,))
            share(1, 2, (part,))
            edge(part + 4, False)
    for offsets in ROUNDS[-DEPTH:]:
        sent_round(me, payload, recv, ss, rs, offsets)
    for offsets in ROUNDS:
        arrived_round(me, payload, recv, ss, rs, offsets)
    for line in up:
        for copy in line:
            copy.wait_send()
    for g in range(2):
        for level in range(3):
            for copy in down[g][level]:
                copy.wait_send()
                if level == 2:
                    copy.wait_recv()
    for copy in halos:
        copy.wait()

    @pl.when(me == LAST)
    def _():
        def done(t, carry):
            rows = pl.ds(first_row(t, "zyx", PIECE), PIECE)
            remote(cand_l.at[rows], glast.at[rows], ls.at[t], lr, t).wait_send()
            return carry

        lax.fori_loop(0, LAST, done, 0)

    own.wait()


def nt(a, b):
    return lax.dot_general(a, b, (((1,), (1,)), ((), ())), preferred_element_type=F32)


def nn(a, b):
    return lax.dot_general(a, b, (((1,), (0,)), ((), ())), preferred_element_type=F32)


def tn(a, b):
    return lax.dot_general(a, b, (((0,), (0,)), ((), ())), preferred_element_type=F32)


def attend_kernel(
    pick, q_ref, k_ref, v_ref, g_ref, halo_ref, other_ref, last_ref, recv,
    out_ref, dq_ref, center_ref, rim_ref, gpart_ref, outgoing,
    rk, rv, tk, tv, bandk, bandv, gk, gv, acck, accv, dsg, pgs, in_sem, out_sem,
):
    me = lax.axis_index("seq")
    h = pl.program_id(0)
    slot = lax.rem(h, 2)
    per_head = QB * RAND

    def load(head, buf):
        for e in range(per_head):
            s = pick[head * per_head + e]
            d, c = lax.div(s, 2), lax.rem(s, 2)
            rows = pl.ds(e * BLOCK, BLOCK)
            pltpu.make_async_copy(recv.at[d, c, 0], rk.at[buf, rows], in_sem.at[buf]).start()
            pltpu.make_async_copy(recv.at[d, c, 1], rv.at[buf, rows], in_sem.at[buf]).start()

    def drain(buf):
        pltpu.make_async_copy(tk.at[buf], tk.at[buf], out_sem.at[buf]).wait()
        pltpu.make_async_copy(tv.at[buf], tv.at[buf], out_sem.at[buf]).wait()

    @pl.when(h == 0)
    def _():
        load(0, 0)

    @pl.when(h + 1 < HEADS_HERE)
    def _():
        load(h + 1, 1 - slot)

    rows_here = QB * BLOCK
    for band, kv, ref in ((bandk, 0, k_ref), (bandv, 1, v_ref)):
        band[0:BLOCK] = halo_ref[0, kv]
        band[BLOCK : BLOCK + rows_here] = ref[...]
        band[BLOCK + rows_here :] = halo_ref[1, kv]
    for g, ref in ((0, other_ref), (1, last_ref)):
        gk[g * BLOCK : (g + 1) * BLOCK] = ref[0, 0]
        gv[g * BLOCK : (g + 1) * BLOCK] = ref[0, 1]
    acck[...] = jnp.zeros_like(acck)
    accv[...] = jnp.zeros_like(accv)
    pltpu.make_async_copy(rk.at[slot], rk.at[slot], in_sem.at[slot]).wait()
    pltpu.make_async_copy(rv.at[slot], rv.at[slot], in_sem.at[slot]).wait()

    @pl.when(h >= 2)
    def _():
        drain(slot)

    span = 3 * BLOCK
    col = lax.broadcasted_iota(jnp.int32, (BLOCK, span), 1)
    for i in range(QB):
        mine = slice(i * BLOCK, (i + 1) * BLOCK)
        q = q_ref[mine, :]
        g = g_ref[mine, :]
        wk, wv = bandk[i * BLOCK : i * BLOCK + span], bandv[i * BLOCK : i * BLOCK + span]
        ek, ev = rk[slot, i * span : (i + 1) * span], rv[slot, i * span : (i + 1) * span]
        sw = nt(q, wk) * SCALE
        if i == 0:
            sw = jnp.where((col < BLOCK) & (me == 0), MASKED, sw)
        if i == QB - 1:
            sw = jnp.where((col >= 2 * BLOCK) & (me == LAST), MASKED, sw)
        sr = nt(q, ek) * SCALE
        sg = nt(q, gk[...]) * SCALE
        peak = jnp.maximum(
            jnp.maximum(jnp.max(sw, axis=1, keepdims=True), jnp.max(sr, axis=1, keepdims=True)),
            jnp.max(sg, axis=1, keepdims=True),
        )
        sw, sr, sg = jnp.exp(sw - peak), jnp.exp(sr - peak), jnp.exp(sg - peak)
        total = (
            jnp.sum(sw, axis=1, keepdims=True)
            + jnp.sum(sr, axis=1, keepdims=True)
            + jnp.sum(sg, axis=1, keepdims=True)
        )
        inverse = 1.0 / total
        sw, sr, sg = sw * inverse, sr * inverse, sg * inverse
        pw, pr, pg = sw.astype(BF), sr.astype(BF), sg.astype(BF)
        out = (nn(pw, wv) + nn(pr, ev) + nn(pg, gv[...])).astype(BF)
        out_ref[mine, :] = out
        delta = jnp.sum(g.astype(F32) * out.astype(F32), axis=1, keepdims=True)
        dw = (sw * (nt(g, wv) - delta)).astype(BF)
        dr = (sr * (nt(g, ev) - delta)).astype(BF)
        dg = (sg * (nt(g, gv[...]) - delta)).astype(BF)
        dq_ref[mine, :] = ((nn(dw, wk) + nn(dr, ek) + nn(dg, gk[...])) * SCALE).astype(BF)
        acck[i * BLOCK : i * BLOCK + span] += tn(dw, q)
        accv[i * BLOCK : i * BLOCK + span] += tn(pw, g)
        tk[slot, i * span : (i + 1) * span] = (tn(dr, q) * SCALE).astype(BF)
        tv[slot, i * span : (i + 1) * span] = tn(pr, g).astype(BF)
        dsg[mine, :] = dg
        pgs[mine, :] = pg
    gdk = tn(dsg[...], q_ref[...]) * SCALE
    gdv = tn(pgs[...], g_ref[...])
    for g in range(2):
        gpart_ref[g, 0, 0] = gdk[g * BLOCK : (g + 1) * BLOCK].astype(BF)
        gpart_ref[g, 0, 1] = gdv[g * BLOCK : (g + 1) * BLOCK].astype(BF)
    center_ref[0] = acck[BLOCK : BLOCK + rows_here] * SCALE
    center_ref[1] = accv[BLOCK : BLOCK + rows_here]
    rim_ref[0, 0] = (acck[0:BLOCK] * SCALE).astype(BF)
    rim_ref[0, 1] = accv[0:BLOCK].astype(BF)
    rim_ref[1, 0] = (acck[BLOCK + rows_here :] * SCALE).astype(BF)
    rim_ref[1, 1] = accv[BLOCK + rows_here :].astype(BF)
    for e in range(per_head):
        s = pick[h * per_head + e]
        d, c = lax.div(s, 2), lax.rem(s, 2)
        rows = pl.ds(e * BLOCK, BLOCK)
        pltpu.make_async_copy(tk.at[slot, rows], outgoing.at[d, c, 0], out_sem.at[slot]).start()
        pltpu.make_async_copy(tv.at[slot, rows], outgoing.at[d, c, 1], out_sem.at[slot]).start()

    @pl.when(h == HEADS_HERE - 1)
    def _():
        drain(1 - slot)
        drain(slot)


def return_kernel(
    outgoing, rim, gpart, returned, rim_back, gother, glast,
    ra, rb, rc, pa, pb, pc, ss, rs, hs, hr, us, ur, ls, lr, bs, br, own_sem,
):
    me = lax.axis_index("seq")
    enter(me)
    after = lax.rem(me + 1, SHARDS)
    before = lax.rem(me + SHARDS - 1, SHARDS)
    own = pltpu.make_async_copy(outgoing.at[0], returned.at[0], own_sem)
    own.start()
    orders = ("yzx", "zyx")
    mine = [pl.ds(first_row(me, order, PIECE), PIECE) for order in orders]
    stages = ((ra, QUART), (rb, 4 * PIECE), (rc, PIECE))
    sums = (pa, pb, pc)

    def reduce_start(g, level, parts=None):
        src = gpart.at[g] if level == 0 else sums[level - 1].at[g]
        dst, rows = stages[level]
        scatter_line(
            me, orders[g][level], src, dst.at[g], rows, us, ur, 12 * g + 4 * level, parts
        )

    def reduce_finish(g, level):
        src = gpart.at[g] if level == 0 else sums[level - 1].at[g]
        dst, rows = stages[level]
        for copy in waits[g][level]:
            copy.wait_recv()
        here = pl.multiple_of(place_of(me, orders[g][level]) * rows, rows)
        total = src[pl.ds(here, rows), :].astype(F32)
        for delta in range(1, 4):
            total = total + dst[g, delta].astype(F32)
        sums[level][g] = total.astype(BF)

    waits = [
        [line_waits(me, ref.at[g], us, ur, 12 * g + 4 * n) for n, (ref, _) in enumerate(stages)]
        for g in range(2)
    ]
    def edge(part, far):
        rows = pl.ds(part * 16, 16)
        for side, target, x in ((0, before, 0), (1, after, 3)):

            @pl.when((place_of(me, "x") == x) == far)
            def _():
                for kv in range(2):
                    remote(
                        rim.at[side, kv, rows], rim_back.at[1 - side, kv, rows],
                        hs.at[2 * side + kv], hr.at[2 * side + kv], target,
                    ).start()

    halos = [
        remote(rim.at[n // 2, n % 2], rim_back.at[n // 2, n % 2], hs.at[n], hr.at[n], me)
        for n in range(4)
    ]
    levels = spread_order(orders[0])
    down = [
        share_waits(me, gother, rows, bs, br, 4 * level) for level, (_, rows) in enumerate(levels)
    ]

    def share(level, parts=None):
        axis, rows = levels[level]
        first = first_row(me, orders[0], rows)
        share_line(me, axis, gother, first, rows, bs, br, 4 * level, parts)

    for part in range(4):
        for g in range(2):
            reduce_start(g, 0, (part,))
        edge(part, False)
    later = []
    for number, offsets in enumerate(ROUNDS):
        if number >= DEPTH:
            sent_round(me, outgoing, returned, ss, rs, ROUNDS[number - DEPTH])
        for step in later:
            step()
        later = []
        send_round(me, -1, outgoing, returned, ss, rs, offsets)
        if number in FAR_AT:
            edge(FAR_AT.index(number), True)
        if number == RETURN_AT[0]:
            for g in range(2):
                reduce_finish(g, 0)
                later.append(functools.partial(reduce_start, g, 1))
        if number == RETURN_AT[1]:
            for g in range(2):
                reduce_finish(g, 1)
                later.append(functools.partial(reduce_start, g, 2))
        if number == RETURN_AT[2]:
            for g in range(2):
                reduce_finish(g, 2)
            gother[mine[0], :] = pc[0]

            def pass_on():
                share(0)

                @pl.when(me != LAST)
                def _():
                    remote(pc.at[1], glast.at[mine[1]], ls, lr.at[me], LAST).start()

            later.append(pass_on)

            @pl.when(me == LAST)
            def _():
                glast[mine[1], :] = pc[1]

        if number == RETURN_AT[3]:
            for copy in down[0]:
                copy.wait_recv()
            share(1)
        if number == RETURN_AT[4]:
            for copy in down[1]:
                copy.wait_recv()
        if RETURN_AT[4] <= number < RETURN_AT[4] + 4:
            part = number - RETURN_AT[4]
            share(2, (part,))
            edge(part + 4, False)
    for offsets in ROUNDS[-DEPTH:]:
        sent_round(me, outgoing, returned, ss, rs, offsets)
    for offsets in ROUNDS:
        arrived_round(me, outgoing, returned, ss, rs, offsets)
    for g in range(2):
        for line in waits[g]:
            for copy in line:
                copy.wait_send()
    for level in range(3):
        for copy in down[level]:
            copy.wait_send()
            if level == 2:
                copy.wait_recv()
    for copy in halos:
        copy.wait()

    @pl.when(me != LAST)
    def _():
        remote(pc.at[1], glast.at[mine[1]], ls, lr.at[me], LAST).wait_send()

    @pl.when(me == LAST)
    def _():
        def done(t, carry):
            rows = pl.ds(first_row(t, "zyx", PIECE), PIECE)
            remote(pc.at[1], glast.at[rows], ls, lr.at[t], t).wait_recv()
            return carry

        lax.fori_loop(0, LAST, done, 0)

    own.wait()


CHUNK = 4


def collect_kernel(
    glob, codes, center, rim, gother, glast, returned, dk_ref, dv_ref, buf, acc, sem, csem
):
    me = lax.axis_index("seq")
    steps = SHARDS // CHUNK

    def fetch(step):
        place = pl.ds(pl.multiple_of(step * CHUNK, CHUNK), CHUNK)
        return pltpu.make_async_copy(returned.at[place], buf.at[place], sem.at[step])

    whole = pltpu.make_async_copy(center, acc, csem)
    whole.start()
    for step in range(steps):
        fetch(step).start()
    whole.wait()
    for kv in range(2):
        acc[kv, 0:BLOCK, :] += rim[0, kv].astype(F32)
        acc[kv, (QB - 1) * BLOCK :, :] += rim[1, kv].astype(F32)

    def add_glob(blk, ref):
        rows = pl.ds(pl.multiple_of(blk * BLOCK, BLOCK), BLOCK)
        for h in range(HEADS_HERE):
            for kv in range(2):
                src = ref[pl.ds((2 * h + kv) * BLOCK, BLOCK), :]
                acc[kv, rows, pl.ds(h * DH, DH)] += src.astype(F32)

    @pl.when(me == LAST)
    def _():
        add_glob(QB - 1, glast)

    other = glob[0] + glob[1] - (SHARDS * QB - 1)

    @pl.when(me == lax.div(other, QB))
    def _():
        add_glob(lax.rem(other, QB), gother)

    def add(code, d, c):
        head = lax.div(code, 4 * QB * RAND)
        blk = lax.rem(code, 4)
        rows = pl.ds(pl.multiple_of(blk * BLOCK, BLOCK), BLOCK)
        cols = pl.ds(pl.multiple_of(head * DH, DH), DH)
        for kv in range(2):
            acc[kv, rows, cols] += buf[d, c, kv].astype(F32)

    def step_body(step, carry):
        fetch(step).wait()
        for place in range(CHUNK):
            d = step * CHUNK + place
            t = moved(me, d)
            low, high = codes[0, t], codes[1, t]

            @pl.when(low < NONE)
            def _():
                add(low, d, 0)

            @pl.when(high > low)
            def _():
                add(high, d, 1)

        return carry

    lax.fori_loop(0, steps, step_body, 0)
    dk_ref[...] = acc[0].astype(BF)
    dv_ref[...] = acc[1].astype(BF)


def smem():
    return pl.BlockSpec(memory_space=pltpu.SMEM)


def vmem():
    return pl.BlockSpec(memory_space=pltpu.VMEM)


def hbm():
    return pl.BlockSpec(memory_space=ANY)


def dma(*shape):
    return pltpu.SemaphoreType.DMA(shape)


def body(queries, keys, values, out_grad, rand_ids, glob_ids):
    place = lax.axis_index("seq")
    group = lax.axis_index("head")
    shape = jax.ShapeDtypeStruct
    ids = lax.dynamic_slice_in_dim(rand_ids, group * HEADS_HERE, HEADS_HERE, 0)
    ids = ids.reshape(HEADS_HERE, SHARDS, QB * RAND)
    own_ids = lax.dynamic_index_in_dim(ids, place, 1, False).reshape(ENTRIES)
    table = ids.transpose(0, 2, 1).reshape(ENTRIES, SHARDS)
    slots = shape((SHARDS, 2, 2, BLOCK, DH), BF)
    grows = shape((GROWS, DH), BF)
    width = HEADS_HERE * DH
    rows_here = QB * BLOCK

    payload, cand_o, cand_l, pick, codes = pl.pallas_call(
        prep_kernel,
        out_shape=(
            slots, grows, grows, shape((ENTRIES,), jnp.int32), shape((2, SHARDS), jnp.int32)
        ),
        in_specs=[smem(), smem(), vmem(), vmem(), vmem()],
        out_specs=(hbm(), hbm(), hbm(), smem(), vmem()),
        scratch_shapes=[
            pltpu.SMEM((SHARDS,), jnp.int32),
            pltpu.SMEM((2, SHARDS), jnp.int32),
            pltpu.SemaphoreType.DMA, dma(2), pltpu.SemaphoreType.DMA,
        ],
        name="prep",
    )(glob_ids, own_ids, table, keys, values)

    recv, halo, gother, glast = pl.pallas_call(
        fetch_kernel,
        out_shape=(slots, shape((2, 2, BLOCK, width), BF), grows, grows),
        in_specs=[smem(), hbm(), hbm(), hbm(), vmem(), vmem()],
        out_specs=(hbm(), hbm(), vmem(), vmem()),
        scratch_shapes=[
            pltpu.VMEM((4, QUART, DH), BF),
            pltpu.VMEM((4, 4 * PIECE, DH), BF),
            pltpu.VMEM((4, PIECE, DH), BF),
            pltpu.VMEM((QUART, DH), BF),
            pltpu.VMEM((4 * PIECE, DH), BF),
            dma(SHARDS), dma(SHARDS), dma(4), dma(4), dma(12), dma(12),
            dma(SHARDS), pltpu.SemaphoreType.DMA, dma(24), dma(24), pltpu.SemaphoreType.DMA,
        ],
        compiler_params=pltpu.CompilerParams(collective_id=0, has_side_effects=True),
        name="fetch",
    )(glob_ids, payload, keys, values, cand_o, cand_l)

    span = 3 * BLOCK
    head_block = pl.BlockSpec((rows_here, DH), lambda h, *_: (0, h))
    side_block = pl.BlockSpec((2, 2, BLOCK, DH), lambda h, *_: (0, 0, 0, h))
    one_block = pl.BlockSpec((1, 2, BLOCK, DH), lambda h, *_: (h, 0, 0, 0))
    glob_block = pl.BlockSpec((2, 1, 2, BLOCK, DH), lambda h, *_: (0, h, 0, 0, 0))
    full = QB * span
    out, dq, center, rim, gpart, outgoing = pl.pallas_call(
        attend_kernel,
        out_shape=(
            shape((rows_here, width), BF),
            shape((rows_here, width), BF),
            shape((2, rows_here, width), F32),
            shape((2, 2, BLOCK, width), BF),
            shape((2, HEADS_HERE, 2, BLOCK, DH), BF),
            slots,
        ),
        grid_spec=pltpu.PrefetchScalarGridSpec(
            num_scalar_prefetch=1,
            grid=(HEADS_HERE,),
            in_specs=[head_block] * 4 + [side_block, one_block, one_block, hbm()],
            out_specs=[
                head_block,
                head_block,
                pl.BlockSpec((2, rows_here, DH), lambda h, *_: (0, 0, h)),
                side_block,
                glob_block,
                hbm(),
            ],
            scratch_shapes=[pltpu.VMEM((2, full, DH), BF)] * 4
            + [pltpu.VMEM((rows_here + 2 * BLOCK, DH), BF)] * 2
            + [pltpu.VMEM((2 * BLOCK, DH), BF)] * 2
            + [pltpu.VMEM((rows_here + 2 * BLOCK, DH), F32)] * 2
            + [pltpu.VMEM((rows_here, 2 * BLOCK), BF)] * 2
            + [dma(2), dma(2)],
        ),
        name="attend",
    )(
        pick, queries, keys, values, out_grad, halo,
        gother.reshape(HEADS_HERE, 2, BLOCK, DH), glast.reshape(HEADS_HERE, 2, BLOCK, DH), recv,
    )

    returned, rim_back, sum_other, sum_last = pl.pallas_call(
        return_kernel,
        out_shape=(slots, shape((2, 2, BLOCK, width), BF), grows, grows),
        in_specs=[hbm(), hbm(), vmem()],
        out_specs=(hbm(), hbm(), vmem(), vmem()),
        scratch_shapes=[
            pltpu.VMEM((2, 4, QUART, DH), BF),
            pltpu.VMEM((2, 4, 4 * PIECE, DH), BF),
            pltpu.VMEM((2, 4, PIECE, DH), BF),
            pltpu.VMEM((2, QUART, DH), BF),
            pltpu.VMEM((2, 4 * PIECE, DH), BF),
            pltpu.VMEM((2, PIECE, DH), BF),
            dma(SHARDS), dma(SHARDS), dma(4), dma(4), dma(24), dma(24),
            pltpu.SemaphoreType.DMA, dma(SHARDS), dma(12), dma(12), pltpu.SemaphoreType.DMA,
        ],
        compiler_params=pltpu.CompilerParams(collective_id=1, has_side_effects=True),
        name="return",
    )(outgoing, rim, gpart.reshape(2, GROWS, DH))

    dk, dv = pl.pallas_call(
        collect_kernel,
        out_shape=(shape((rows_here, width), BF), shape((rows_here, width), BF)),
        in_specs=[smem(), smem(), hbm(), vmem(), vmem(), vmem(), hbm()],
        out_specs=(vmem(), vmem()),
        scratch_shapes=[
            pltpu.VMEM((SHARDS, 2, 2, BLOCK, DH), BF),
            pltpu.VMEM((2, rows_here, width), F32),
            dma(SHARDS // CHUNK),
            pltpu.SemaphoreType.DMA,
        ],
        name="collect",
    )(glob_ids, codes, center, rim_back, sum_other, sum_last, returned)
    return out, dq, dk, dv


def solution(mesh):
    rows = P("seq", "head")
    return jax.shard_map(
        body,
        mesh=mesh,
        in_specs=(rows, rows, rows, rows, P(), P()),
        out_specs=(rows, rows, rows, rows),
        check_vma=False,
    )
```

time: 399 us -> 381 us (0.955)
  other arithmetic: 12.5 us -> 0 us
  Pallas kernels: 377 us -> 373 us
    pallas_call x1, Pallas kernels: 160 us -> 133 us  [body(): pl.pallas_call(fetch_kernel, out_shape=(slots, shape((2, 2, BLOCK, width)...]
    pallas_call x1, Pallas kernels: 159 us -> 183 us  [body(): pl.pallas_call(return_kernel, out_shape=(slots, shape((2, 2, BLOCK, width...]
    reduce_max x2 -> x0, other arithmetic: 9.81 us -> none  [body(): cmax = jnp.max(jnp.where(hit, code, -1), axis=(0, 2))]
    pallas_call x1, Pallas kernels: 15.8 us -> 11.7 us  [body(): pl.pallas_call(collect_kernel, out_shape=(shape((rows_here, width), BF),...]
where the time goes in v2:
time: 381 us; the launch traced here: 377 us
  Pallas kernels  373 us (98%)
    pallas_call x1, Pallas kernels, body(): pl.pallas_call(return_kernel, out_shape=(slots, shape((2, 2, BLOCK, width...  183 us
    pallas_call x1, Pallas kernels, body(): pl.pallas_call(fetch_kernel, out_shape=(slots, shape((2, 2, BLOCK, width)...  133 us
    pallas_call x1, Pallas kernels, body(): pl.pallas_call(attend_kernel, out_shape=(shape((rows_here, width), BF), s...  37.2 us
    pallas_call x1, Pallas kernels, body(): pl.pallas_call(collect_kernel, out_shape=(shape((rows_here, width), BF),...  11.7 us

profile of v2, /device:TPU:34, one launch (start us, length us, event | category | flops | bytes accessed | tf_op | source)
XLA Modules:
  0.0 376.7 jit_solution(17041154318932549124)
XLA Ops:
  0.6 0.0 copy-start
  0.7 0.8 copy-done
  1.4 0.2 copy.11
  1.7 0.2 reshape.27
  1.9 0.1 copy.12
  2.0 0.6 reshape.28.own_ids
  2.6 0.3 copy.13
  2.8 0.6 reshape.29.ids
  3.4 7.5 %prep.1 = (bf16[64,2,2,128,128]{4,3,2,1,0:T(8,128)(2,1)}, bf16[2048,128]{1,0:T(8,128)(2,1)}, bf16[2048,128]{1,0:T(8,128)(2,1)}, s32[96]{0:T(128)}, s32[2,64]{1,0:T(2,128)}) custom-call(s32[2]{0:T(128)} %glob.5, s32[96]{0:T(128)} %reshape.28.own_ids, s32[96,64]{1,0:T(8,128)} %reshape.29.ids, bf16[512,1024]{1,0:T(8,128)(2,1)} %k_ref.5, bf16[512,1024]{1,0:T(8,128)(2,1)} %v_ref.5), custom_call_target="tpu_custom_call" | custom-call | tf_op jit(solution)/shard_map/prep/pallas_call | solution.py:758
  11.0 133.5 %fetch.1 = (bf16[64,2,2,128,128]{4,3,2,1,0:T(8,128)(2,1)}, bf16[2,2,128,1024]{3,2,1,0:T(8,128)(2,1)}, bf16[2048,128]{1,0:T(8,128)(2,1)}, bf16[2048,128]{1,0:T(8,128)(2,1)}) custom-call(s32[2]{0:T(128)} %glob.5, bf16[64,2,2,128,128]{4,3,2,1,0:T(8,128)(2,1)} %get-tuple-element.26.payload, bf16[512,1024]{1,0:T(8,128)(2,1)} %k_ref.5, bf16[512,1024]{1,0:T(8,128)(2,1)} %v_ref.5, ...), custom_call_target="tpu_custom_call" | custom-call | tf_op jit(solution)/shard_map/fetch/pallas_call | solution.py:773
  144.4 37.2 %attend.1 = (bf16[512,1024]{1,0:T(8,128)(2,1)}, bf16[512,1024]{1,0:T(8,128)(2,1)}, f32[2,512,1024]{2,1,0:T(8,128)}, bf16[2,2,128,1024]{3,2,1,0:T(8,128)(2,1)}, b...) custom-call(s32[96]{0:T(128)} %get-tuple-element.25.pick, bf16[512,1024]{1,0:T(8,128)(2,1)} %q_ref.1, ...), custom_call_target="tpu_custom_call" | custom-call | tf_op jit(solution)/shard_map/attend/pallas_call | solution.py:797
  181.7 183.3 %return.1 = (bf16[64,2,2,128,128]{4,3,2,1,0:T(8,128)(2,1)}, bf16[2,2,128,1024]{3,2,1,0:T(8,128)(2,1)}, bf16[2048,128]{1,0:T(8,128)(2,1)}, bf16[2048,128]{1,0:T(8,128)(2,1)}) custom-call(bf16[64,2,2,128,128]{4,3,2,1,0:T(8,128)(2,1)} %get-tuple-element.37.outgoing, bf16[2,2,128,1024]{3,2,1,0:T(8,128)(2,1)} %get-tuple-element.38.rim, bf16[2,2048,128]{2,1,0:T(8,128)(2,1)} %bitcast.9), custom_call_target="tpu_custom_call" | custom-call | tf_op jit(solution)/shard_map/return/pallas_call | solution.py:832
  365.0 11.7 %collect.1 = (bf16[512,1024]{1,0:T(8,128)(2,1)}, bf16[512,1024]{1,0:T(8,128)(2,1)}) custom-call(s32[2]{0:T(128)} %glob.5, s32[2,64]{1,0:T(2,128)} %get-tuple-element.35.codes, f32[2,512,1024]{2,1,0:T(8,128)} %get-tuple-element.36.center, bf16[2,2,128,1024]{3,2,1,0:T(8,128)(2,1)} %get-tuple-element.40.rim, bf16[2048,128]{1,0:T(8,128)(2,1)} %get-tuple-element.41.gother, ...), custom_call_target="tpu_custom_call" | custom-call | tf_op jit(solution)/shard_map/collect/pallas_call | solution.py:851
  (2 shorter events, 0.0 us)
Async XLA Ops:
  0.6 0.8 copy-start

commit v3 on v2

--- a/solution.py
+++ b/solution.py
@@ -17,9 +17,10 @@
 ENTRIES = HEADS_HERE * QB * RAND
 NONE = 1 << 20
 DEPTH = 6
-FETCH_AT = (1, 2, 3, 4, 8)
-FAR_AT = (1, 2, 3, 4, 5, 6, 7, 8)
-RETURN_AT = (3, 4, 5, 6, 8)
+FETCH_AT = (1, 3, 5, 8, 9)
+FETCH_FAR = (0, 1, 2, 3, 5, 6, 9, 11)
+RETURN_FAR = (1, 2, 3, 4, 5, 6, 7, 8)
+RETURN_AT = (3, 4, 5, 6, 7)
 LAST = SHARDS - 1
 GROWS = HEADS_HERE * 2 * BLOCK
 PIECE = GROWS // SHARDS
@@ -316,8 +317,8 @@
             step()
         later = []
         send_round(me, 1, payload, recv, ss, rs, offsets)
-        if number in FAR_AT:
-            edge(FAR_AT.index(number), True)
+        if number in FETCH_FAR:
+            edge(FETCH_FAR.index(number), True)
         if number == FETCH_AT[0]:
             for copy in up[0]:
                 copy.wait_recv()
@@ -574,6 +575,34 @@
         first = first_row(me, orders[0], rows)
         share_line(me, axis, gother, first, rows, bs, br, 4 * level, parts)
 
+    tree = spread_order(orders[1])
+
+    def on_path(level):
+        ok = me >= 0
+        for axis, _ in tree[:level]:
+            ok = ok & (place_of(me, axis) == 3)
+        return ok
+
+    def is_sender(level):
+        return on_path(level) & (place_of(me, tree[level][0]) != 3)
+
+    def gather_copy(level, source):
+        axis, rows = tree[level]
+        ref = glast.at[pl.ds(first_row(me, orders[1], rows), rows)]
+        target = me + (3 - place_of(me, axis)) * STEP[axis]
+        return remote(ref, ref, ls.at[level], lr.at[4 * level + source], target)
+
+    def gather_send(level):
+        @pl.when(is_sender(level))
+        def _():
+            gather_copy(level, place_of(me, tree[level][0])).start()
+
+    def gather_take(level):
+        @pl.when(on_path(level + 1))
+        def _():
+            for source in range(3):
+                gather_copy(level, source).wait_recv()
+
     for part in range(4):
         for g in range(2):
             reduce_start(g, 0, (part,))
@@ -586,8 +615,8 @@
             step()
         later = []
         send_round(me, -1, outgoing, returned, ss, rs, offsets)
-        if number in FAR_AT:
-            edge(FAR_AT.index(number), True)
+        if number in RETURN_FAR:
+            edge(RETURN_FAR.index(number), True)
         if number == RETURN_AT[0]:
             for g in range(2):
                 reduce_finish(g, 0)
@@ -603,24 +632,21 @@
 
             def pass_on():
                 share(0)
-
-                @pl.when(me != LAST)
-                def _():
-                    remote(pc.at[1], glast.at[mine[1]], ls, lr.at[me], LAST).start()
+                gather_send(0)
 
             later.append(pass_on)
-
-            @pl.when(me == LAST)
-            def _():
-                glast[mine[1], :] = pc[1]
-
+            glast[mine[1], :] = pc[1]
         if number == RETURN_AT[3]:
             for copy in down[0]:
                 copy.wait_recv()
+            gather_take(0)
             share(1)
+            gather_send(1)
         if number == RETURN_AT[4]:
             for copy in down[1]:
                 copy.wait_recv()
+            gather_take(1)
+            gather_send(2)
         if RETURN_AT[4] <= number < RETURN_AT[4] + 4:
             part = number - RETURN_AT[4]
             share(2, (part,))
@@ -641,19 +667,13 @@
     for copy in halos:
         copy.wait()
 
-    @pl.when(me != LAST)
-    def _():
-        remote(pc.at[1], glast.at[mine[1]], ls, lr.at[me], LAST).wait_send()
-
-    @pl.when(me == LAST)
-    def _():
-        def done(t, carry):
-            rows = pl.ds(first_row(t, "zyx", PIECE), PIECE)
-            remote(pc.at[1], glast.at[rows], ls, lr.at[t], t).wait_recv()
-            return carry
-
-        lax.fori_loop(0, LAST, done, 0)
-
+    for level in range(3):
+
+        @pl.when(is_sender(level))
+        def _():
+            gather_copy(level, 0).wait_send()
+
+    gather_take(2)
     own.wait()
 
 
@@ -842,7 +862,7 @@
             pltpu.VMEM((2, 4 * PIECE, DH), BF),
             pltpu.VMEM((2, PIECE, DH), BF),
             dma(SHARDS), dma(SHARDS), dma(4), dma(4), dma(24), dma(24),
-            pltpu.SemaphoreType.DMA, dma(SHARDS), dma(12), dma(12), pltpu.SemaphoreType.DMA,
+            dma(3), dma(12), dma(12), dma(12), pltpu.SemaphoreType.DMA,
         ],
         compiler_params=pltpu.CompilerParams(collective_id=1, has_side_effects=True),
         name="return",

time: 381 us -> 377 us (0.990); the launches traced: 377 us -> 377 us
    pallas_call x1, Pallas kernels: 183 us -> 194 us  [body(): pl.pallas_call(return_kernel, out_shape=(slots, shape((2, 2, BLOCK, width...]
    pallas_call x1, Pallas kernels: 133 us -> 123 us  [body(): pl.pallas_call(fetch_kernel, out_shape=(slots, shape((2, 2, BLOCK, width)...]
where the time goes in v3:
time: 377 us
  Pallas kernels  374 us (99%)
    pallas_call x1, Pallas kernels, body(): pl.pallas_call(return_kernel, out_shape=(slots, shape((2, 2, BLOCK, width...  194 us
    pallas_call x1, Pallas kernels, body(): pl.pallas_call(fetch_kernel, out_shape=(slots, shape((2, 2, BLOCK, width)...  123 us
    pallas_call x1, Pallas kernels, body(): pl.pallas_call(attend_kernel, out_shape=(shape((rows_here, width), BF), s...  37.2 us
    pallas_call x1, Pallas kernels, body(): pl.pallas_call(collect_kernel, out_shape=(shape((rows_here, width), BF),...  12 us

profile of v3, /device:TPU:34, one launch (start us, length us, event | category | flops | bytes accessed | tf_op | source)
XLA Modules:
  0.0 377.3 jit_solution(6814825702010661304)
XLA Ops:
  0.6 0.0 copy-start
  0.7 0.8 copy-done
  1.4 0.2 copy.11
  1.7 0.2 reshape.27
  1.9 0.1 copy.12
  2.0 0.6 reshape.28.own_ids
  2.6 0.3 copy.13
  2.8 0.6 reshape.29.ids
  3.4 7.5 %prep.1 = (bf16[64,2,2,128,128]{4,3,2,1,0:T(8,128)(2,1)}, bf16[2048,128]{1,0:T(8,128)(2,1)}, bf16[2048,128]{1,0:T(8,128)(2,1)}, s32[96]{0:T(128)}, s32[2,64]{1,0:T(2,128)}) custom-call(s32[2]{0:T(128)} %glob.5, s32[96]{0:T(128)} %reshape.28.own_ids, s32[96,64]{1,0:T(8,128)} %reshape.29.ids, bf16[512,1024]{1,0:T(8,128)(2,1)} %k_ref.5, bf16[512,1024]{1,0:T(8,128)(2,1)} %v_ref.5), custom_call_target="tpu_custom_call" | custom-call | tf_op jit(solution)/shard_map/prep/pallas_call | solution.py:778
  11.0 122.9 %fetch.1 = (bf16[64,2,2,128,128]{4,3,2,1,0:T(8,128)(2,1)}, bf16[2,2,128,1024]{3,2,1,0:T(8,128)(2,1)}, bf16[2048,128]{1,0:T(8,128)(2,1)}, bf16[2048,128]{1,0:T(8,128)(2,1)}) custom-call(s32[2]{0:T(128)} %glob.5, bf16[64,2,2,128,128]{4,3,2,1,0:T(8,128)(2,1)} %get-tuple-element.26.payload, bf16[512,1024]{1,0:T(8,128)(2,1)} %k_ref.5, bf16[512,1024]{1,0:T(8,128)(2,1)} %v_ref.5, ...), custom_call_target="tpu_custom_call" | custom-call | tf_op jit(solution)/shard_map/fetch/pallas_call | solution.py:793
  133.9 37.2 %attend.1 = (bf16[512,1024]{1,0:T(8,128)(2,1)}, bf16[512,1024]{1,0:T(8,128)(2,1)}, f32[2,512,1024]{2,1,0:T(8,128)}, bf16[2,2,128,1024]{3,2,1,0:T(8,128)(2,1)}, b...) custom-call(s32[96]{0:T(128)} %get-tuple-element.25.pick, bf16[512,1024]{1,0:T(8,128)(2,1)} %q_ref.1, ...), custom_call_target="tpu_custom_call" | custom-call | tf_op jit(solution)/shard_map/attend/pallas_call | solution.py:817
  171.1 194.2 %return.1 = (bf16[64,2,2,128,128]{4,3,2,1,0:T(8,128)(2,1)}, bf16[2,2,128,1024]{3,2,1,0:T(8,128)(2,1)}, bf16[2048,128]{1,0:T(8,128)(2,1)}, bf16[2048,128]{1,0:T(8,128)(2,1)}) custom-call(bf16[64,2,2,128,128]{4,3,2,1,0:T(8,128)(2,1)} %get-tuple-element.37.outgoing, bf16[2,2,128,1024]{3,2,1,0:T(8,128)(2,1)} %get-tuple-element.38.rim, bf16[2,2048,128]{2,1,0:T(8,128)(2,1)} %bitcast.9), custom_call_target="tpu_custom_call" | custom-call | tf_op jit(solution)/shard_map/return/pallas_call | solution.py:852
  365.3 12.0 %collect.1 = (bf16[512,1024]{1,0:T(8,128)(2,1)}, bf16[512,1024]{1,0:T(8,128)(2,1)}) custom-call(s32[2]{0:T(128)} %glob.5, s32[2,64]{1,0:T(2,128)} %get-tuple-element.35.codes, f32[2,512,1024]{2,1,0:T(8,128)} %get-tuple-element.36.center, bf16[2,2,128,1024]{3,2,1,0:T(8,128)(2,1)} %get-tuple-element.40.rim, bf16[2048,128]{1,0:T(8,128)(2,1)} %get-tuple-element.41.gother, ...), custom_call_target="tpu_custom_call" | custom-call | tf_op jit(solution)/shard_map/collect/pallas_call | solution.py:871
  (2 shorter events, 0.0 us)
Async XLA Ops:
  0.6 0.8 copy-start
